TPU v7x, 32 devices: a whole 2x2x4 slice. The times are simulated.
32 devices in a mesh: row: 8 (over z, core), col: 4 (over y, x).
Axes of the slice: x: 2, y: 2, z: 4, core: 2. Of those that a mesh axis runs over, the one named last changes fastest.
Arguments:
- density_owned: float32 [8, 4, 4, 512, 512], P('row', 'col'), may hold values from -0.125 to 0.125
- hamilton_owned: float32 [8, 4, 3, 512, 512], P('row', 'col'), may hold values from -6 to 6
- density_route: int32 [8, 4, 4, 2], P('row', 'col'), may hold values from 0 to 7, as said below
- hamilton_route: int32 [8, 4, 3, 2], P('row', 'col'), may hold values from 0 to 7, as said below
- pair_lists: int32 [8, 4, 3, 12, 3], P('row', 'col'), may hold values from 0 to 5, as said below
- pair_counts: int32 [8, 4, 3], P('row', 'col'), may hold values from 4 to 12, as said below
Outputs:
- product: float32 [8, 4, 4, 512, 512], P('row', 'col')
Inputs may be any that keep to these rules, and one draw needn't show every extreme that they name: `density_route`: entry (t, u): the grid row t in the owner's own grid column that takes the block and its slot u there. Every grid device takes exactly one density block for each of its 4 slots and one Hamiltonian block for each of its 3 slots, and the 7 blocks of one owner go to different grid rows. `hamilton_route`: as for density_route; the Hamiltonian slot u is below 3. `pair_lists`: entry (x, y, o): x below 4, y below 6, o below 4; the first 4 entries of each list name every product slot once. Only the first pair_counts[i, j, s] entries of list (i, j, s) count; at every stop some grid device has 12.
All inputs are finite; a program needn't handle non-finite values.
Results may differ from a plain program's by a relative error of at most 0.0003.
Values sent between devices are 32-bit elements; how exact they have to be, the bound alone decides.
No kernel may reach another device: no remote copies, remote signals or barrier semaphores. Data moves between devices by JAX's collectives and lax.ppermute only.
A program may use at most 128 MiB of HBM per device.

v0:
```python
import functools

import jax
import jax.numpy as jnp
from jax import lax
from jax.experimental import pallas as pl
from jax.experimental.pallas import tpu as pltpu
from jax.sharding import PartitionSpec as P


OUT = 4
STOPS = 3
LAST = 1
NOTE = 8
CORES = 2


def from_behind(block, axis, distance):
    size = lax.axis_size(axis)
    return lax.ppermute(block, axis, [((i - distance) % size, i) for i in range(size)])


def split(x):
    high = x.astype(jnp.bfloat16)
    low = (x - high.astype(jnp.float32)).astype(jnp.bfloat16)
    return high, low


def product(left, right):
    lh, ll = split(left)
    rh, rl = split(right)
    dot = functools.partial(jnp.dot, preferred_element_type=jnp.float32)
    return dot(lh, rh) + (dot(lh, rl) + dot(ll, rh))


def pairs_kernel(phase, n_left, n_right, fresh, table, *refs):
    lefts = refs[:n_left]
    rights = refs[n_left:n_left + n_right]
    rest = refs[n_left + n_right:]
    if fresh:
        out, todo, lbuf, rbuf, lsem, rsem = rest
        out[...] = jnp.zeros_like(out)
    else:
        before, out, todo, lbuf, rbuf, lsem, rsem = rest
        out[...] = before[...]

    def pick(p, count):
        mine = table[5, p] == phase

        @pl.when(mine)
        def _():
            todo[count] = p

        return count + mine.astype(jnp.int32)

    count = lax.fori_loop(0, table.shape[1], pick, jnp.int32(0))

    def fetch(position, slot):
        p = todo[position]
        for k, ref in enumerate(lefts):
            @pl.when(table[0, p] == k)
            def _(ref=ref):
                pltpu.make_async_copy(ref.at[table[1, p]], lbuf.at[slot], lsem.at[slot]).start()
        for k, ref in enumerate(rights):
            @pl.when(table[2, p] == k)
            def _(ref=ref):
                pltpu.make_async_copy(ref.at[table[3, p]], rbuf.at[slot], rsem.at[slot]).start()

    @pl.when(count > 0)
    def _():
        fetch(0, 0)

    def step(position, carry):
        slot = lax.rem(position, 2)

        @pl.when(position + 1 < count)
        def _():
            fetch(position + 1, 1 - slot)

        pltpu.make_async_copy(lefts[0].at[0], lbuf.at[slot], lsem.at[slot]).wait()
        pltpu.make_async_copy(rights[0].at[0], rbuf.at[slot], rsem.at[slot]).wait()
        o = table[4, todo[position]]
        out[o] += product(lbuf[slot], rbuf[slot])
        return carry

    lax.fori_loop(0, count, step, 0)


def run_pairs(phase, table, lefts, rights, before, out_shape):
    n_left, n_right = len(lefts), len(rights)
    width = out_shape[-1]
    any_spec = pl.BlockSpec(memory_space=pl.ANY)
    whole = pl.BlockSpec(memory_space=pltpu.VMEM)
    fresh = before is None
    ins = list(lefts) + list(rights) + ([] if fresh else [before])
    specs = [any_spec] * (n_left + n_right) + ([] if fresh else [whole])
    work = 10 * width ** 3
    return pl.pallas_call(
        functools.partial(pairs_kernel, phase, n_left, n_right, fresh),
        out_shape=jax.ShapeDtypeStruct(out_shape, jnp.float32),
        grid_spec=pltpu.PrefetchScalarGridSpec(
            num_scalar_prefetch=1,
            grid=(),
            in_specs=specs,
            out_specs=whole,
            scratch_shapes=[
                pltpu.SMEM((table.shape[1],), jnp.int32),
                pltpu.VMEM((2, width, width), jnp.float32),
                pltpu.VMEM((2, width, width), jnp.float32),
                pltpu.SemaphoreType.DMA((2,)),
                pltpu.SemaphoreType.DMA((2,)),
            ],
        ),
        compiler_params=pltpu.CompilerParams(vmem_limit_bytes=32 << 20),
        cost_estimate=pl.CostEstimate(flops=6 * work, bytes_accessed=20 * width * width * 4, transcendentals=0),
    )(table, *ins)


def pack_kernel(d_route, h_route, dens, sent, blocks, notes, in_sem, out_sem, note_sem):
    count, width = dens.shape[0], dens.shape[1]
    rows = sent.shape[0]
    for q in range(count):
        pltpu.make_async_copy(dens.at[q], blocks.at[q], in_sem.at[q]).start()
    lane = lax.broadcasted_iota(jnp.int32, notes.shape[1:], 1)
    shared = jnp.full(notes.shape[1:], -1.0, jnp.float32)
    for k in range(h_route.shape[0]):
        shared = jnp.where(lane == k + 1, h_route[k].astype(jnp.float32), shared)
    for t in range(rows):
        notes[t] = shared
    for q in range(count):
        notes[d_route[2 * q]] = jnp.where(lane == 0, d_route[2 * q + 1].astype(jnp.float32), shared)
    note_copy = pltpu.make_async_copy(notes, sent.at[:, pl.ds(width, NOTE), :], note_sem)
    note_copy.start()
    outs = []
    for q in range(count):
        pltpu.make_async_copy(dens.at[q], blocks.at[q], in_sem.at[q]).wait()
        out = pltpu.make_async_copy(blocks.at[q], sent.at[d_route[2 * q], pl.ds(0, width), :], out_sem.at[q])
        out.start()
        outs.append(out)
    for out in outs:
        out.wait()
    note_copy.wait()


def pack(d_route, h_route, dens, rows):
    count, width = dens.shape[0], dens.shape[1]
    return pl.pallas_call(
        pack_kernel,
        out_shape=jax.ShapeDtypeStruct((rows, width + NOTE, width), jnp.float32),
        grid_spec=pltpu.PrefetchScalarGridSpec(
            num_scalar_prefetch=2,
            grid=(),
            in_specs=[pl.BlockSpec(memory_space=pl.ANY)],
            out_specs=pl.BlockSpec(memory_space=pl.ANY),
            scratch_shapes=[
                pltpu.VMEM(dens.shape, jnp.float32),
                pltpu.VMEM((rows, NOTE, width), jnp.float32),
                pltpu.SemaphoreType.DMA((count,)),
                pltpu.SemaphoreType.DMA((count,)),
                pltpu.SemaphoreType.DMA,
            ],
        ),
        cost_estimate=pl.CostEstimate(flops=0, bytes_accessed=8 * count * width * width, transcendentals=0),
        name="pack",
    )(d_route, h_route, dens)


def gathered(*args):
    return gathered_product(*args)


def gathered_product(density_owned, hamilton_owned, density_route, hamilton_route, pair_lists, pair_counts):
    rows, cols = lax.axis_size("row"), lax.axis_size("col")
    row, col = lax.axis_index("row"), lax.axis_index("col")
    left_count, half_count, width = density_owned.shape[2], hamilton_owned.shape[2], density_owned.shape[3]
    half = rows // 2
    c = CORES
    dens, ham = density_owned[0, 0], hamilton_owned[0, 0]

    def chips(moves):
        return [(a * c + k, b * c + k) for a, b in moves for k in range(c)]

    inward = chips([(0, 1), (3, 2)])
    mid = chips([(1, 2), (2, 1)])
    outward = chips([(1, 0), (2, 3)])
    swap_all = [(i, i ^ 1) for i in range(rows)]
    swap_mid = [(i, i ^ 1) for i in range(c, rows - c)]
    swap_end = [(i, i ^ 1) for i in range(rows) if i < c or i >= rows - c]
    n_far = 2 * half_count

    def move(block, pairs, axis="row"):
        return lax.ppermute(block, axis, pairs)

    beside_out = move(ham, outward)
    own_x = move(ham, swap_all)

    grid_rows = jnp.arange(rows, dtype=jnp.int32)
    sent = pack(density_route[0, 0].reshape(-1), hamilton_route[0, 0].reshape(-1), dens, rows)
    arrived = lax.all_to_all(sent, "row", split_axis=0, concat_axis=0, tiled=True)
    notes = arrived[:, width, :1 + 2 * half_count].astype(jnp.int32)

    blocks = [ham[q:q + 1] for q in range(half_count)]
    beside_in = [move(block, inward) for block in blocks]
    beside_in_x = [move(block, swap_mid) for block in beside_in]
    beside_out_x = move(beside_out, swap_end)

    slot_of = notes[:, 0]
    source = jnp.sum(
        (slot_of[None, :] == jnp.arange(left_count, dtype=jnp.int32)[:, None]).astype(jnp.int32) * grid_rows[None, :], axis=1)
    tile = [lax.dynamic_slice(arrived, (source[b], 0, 0), (1, width, width)) for b in range(left_count)]
    two_on = [((j + 2) % cols, j) for j in range(cols)]
    odd_to_even = [(j + 1, j) for j in range(0, cols, 2)]
    even_to_odd = [(j, j + 1) for j in range(0, cols, 2)]
    after_two = [move(t, two_on, "col") for t in tile]
    after_one_even = [move(t, odd_to_even, "col") for t in tile]
    after_one_odd = [move(t, even_to_odd, "col") for t in after_two]

    far_mid, far_out, far_mid_x, far_out_x = [], [], [], []
    for f in range(n_far):
        far_mid.append(move((blocks + beside_in)[f], mid))
        far_out.append(move(far_mid[f], outward))
        far_mid_x.append(move(far_mid[f], swap_mid))
        far_out_x.append(move(far_out[f], swap_end))

    stops, pairs = pair_lists.shape[2], pair_lists.shape[3]
    total = stops * pairs
    listing = pair_lists[0, 0].reshape(total, 3)
    stop = jnp.arange(total, dtype=jnp.int32) // pairs
    live = (jnp.arange(total, dtype=jnp.int32) % pairs) < jnp.repeat(pair_counts[0, 0], pairs, total_repeat_length=total)
    x, y, o = listing[:, 0], listing[:, 1], listing[:, 2]
    is_odd = col % 2
    group = jnp.where(stop == 0, 0, jnp.where(stop == 2, 1, 2 + is_odd))
    left_ref = group * left_count + x
    left_pos = jnp.zeros_like(left_ref)
    wanted = ((row + stop) % half + jnp.where(y >= half_count, half, 0)) * half_count + y % half_count
    routes = notes[:, 1:].reshape(rows * half_count, 2)
    target = routes[:, 0] * half_count + routes[:, 1]
    owner_code = jnp.sum(
        (target[None, :] == wanted[:, None]).astype(jnp.int32)
        * jnp.arange(rows * half_count, dtype=jnp.int32)[None, :], axis=1)
    owner, q = owner_code // half_count, owner_code % half_count
    chip, owner_chip = row // c, owner // c
    crossed = (owner % c != row % c).astype(jnp.int32)
    same = owner_chip == chip
    paired = owner_chip // 2 == chip // 2
    inner = jnp.logical_or(owner_chip == 1, owner_chip == 2)
    far_index = jnp.where(inner, 0, half_count) + q
    i_am_inner = jnp.logical_or(chip == 1, chip == 2)
    near_refs = 4 + 2 * half_count
    far_ref = near_refs + jnp.where(i_am_inner, 0, 2 * n_far) + crossed * n_far + far_index
    beside_ref = jnp.where(i_am_inner, 4 + crossed * half_count + q, 2 + crossed)
    right_ref = jnp.where(same, crossed, jnp.where(paired, beside_ref, far_ref))
    right_pos = jnp.where(jnp.logical_and(paired, right_ref < 4), q, 0)
    cut = n_far - LAST
    late = jnp.logical_and(jnp.logical_not(paired), far_index >= cut)
    phase = jnp.where(live, late.astype(jnp.int32), -1)
    far_group, far_place = (right_ref - near_refs) // n_far, (right_ref - near_refs) % n_far
    early_ref = jnp.where(right_ref < near_refs, right_ref, near_refs + far_group * cut + far_place)
    late_ref = far_group * LAST + far_place - cut
    table = jnp.stack([left_ref, left_pos, jnp.where(late, late_ref, early_ref), right_pos, o, phase], axis=0)

    lefts = tile + after_two + after_one_even + after_one_odd
    far = [far_mid, far_mid_x, far_out, far_out_x]
    early_rights = [ham, own_x, beside_out, beside_out_x] + beside_in + beside_in_x + [r for g in far for r in g[:cut]]
    late_rights = [r for g in far for r in g[cut:]]
    shape = (OUT, width, width)
    result = run_pairs(0, table, lefts, early_rights, None, shape)
    result = run_pairs(1, table, lefts, late_rights, result, shape)
    return result[None, None]


def stop_products(total, left_tile, right_tile, listing, live):

    def add_pair(position, running):
        entry = listing[position]
        left_block = lax.dynamic_index_in_dim(left_tile, entry[0], 0, keepdims=False)
        right_block = lax.dynamic_index_in_dim(right_tile, entry[1], 0, keepdims=False)
        term = jnp.dot(left_block, right_block, precision=lax.Precision.HIGHEST, preferred_element_type=jnp.float32)
        current = lax.dynamic_index_in_dim(running, entry[2], 0, keepdims=False)
        return lax.dynamic_update_index_in_dim(running, current + term, entry[2], 0)

    return lax.fori_loop(0, live, add_pair, total)


def shifted(density_owned, hamilton_owned, density_route, hamilton_route, pair_lists, pair_counts):
    rows = lax.axis_size("row")
    my_row = lax.axis_index("row")
    half = rows // 2
    left_count, half_count, width = density_owned.shape[2], hamilton_owned.shape[2], density_owned.shape[3]
    owned = jnp.concatenate([density_owned[0, 0], hamilton_owned[0, 0]], axis=0)
    targets = jnp.concatenate([density_route[0, 0, :, 0], hamilton_route[0, 0, :, 0]])
    labels = jnp.concatenate([density_route[0, 0, :, 1], hamilton_route[0, 0, :, 1] + left_count])
    send_blocks = jnp.zeros((rows, width, width), jnp.float32).at[targets].set(owned)
    send_labels = jnp.full((rows,), -1, jnp.int32).at[targets].set(labels)
    arrived, arrived_labels = (
        lax.all_to_all(send_blocks, "row", split_axis=0, concat_axis=0, tiled=True),
        lax.all_to_all(send_labels, "row", split_axis=0, concat_axis=0, tiled=True),
    )
    wanted = jnp.arange(left_count + half_count, dtype=jnp.int32)
    matches = (arrived_labels[None, :] == wanted[:, None]).astype(jnp.int32)
    sources = jnp.sum(matches * jnp.arange(rows, dtype=jnp.int32)[None, :], axis=1)
    placed = arrived[sources]
    left_tile = placed[:left_count]
    own_half = placed[left_count:]
    other_half = from_behind(own_half, "row", half)
    right_tile = jnp.where(
        my_row < half,
        jnp.concatenate([own_half, other_half], axis=0),
        jnp.concatenate([other_half, own_half], axis=0),
    )
    result = jnp.zeros((OUT, width, width), jnp.float32)
    for stop_index in range(STOPS):
        result = stop_products(
            result, left_tile, right_tile, pair_lists[0, 0, stop_index], pair_counts[0, 0, stop_index])
        if stop_index + 1 < STOPS:
            left_tile = from_behind(left_tile, "col", -1)
            right_tile = from_behind(right_tile, "row", -1)
    return result[None, None]


def solution(mesh):
    rows, cols = mesh.shape["row"], mesh.shape["col"]
    lined = rows == CORES * (STOPS + 1) and cols % 2 == 0
    return jax.shard_map(
        gathered if lined else shifted,
        mesh=mesh,
        in_specs=(
            P("row", "col", None, None, None),
            P("row", "col", None, None, None),
            P("row", "col", None, None),
            P("row", "col", None, None),
            P("row", "col", None, None, None),
            P("row", "col", None),
        ),
        out_specs=P("row", "col", None, None, None),
        check_vma=False,
    )
```

profile of v0, /device:TPU:0, one launch (start us, length us, event | category | flops | bytes accessed | tf_op | source)
XLA Modules:
  0.0 689.5 jit_solution(10608963179273327239)
XLA Ops:
  2.7 4.1 pack.1
  6.8 6.3 all-to-all-start
  13.1 2.2 slice_bitcast_fusion
  15.3 4.0 collective-permute-start.20
  19.3 1.4 collective-permute-start.21
  22.9 151.0 %collective-permute-done.20.refs_20_ = f32[1,512,512]{2,1,0:T(8,128)S(1)} collective-permute-done((f32[1,512,512]{2,1,0:T(8,128)S(1)}, f32[1,512,512]{2,1,0:T(8,128)S(1)}, u32[]{:S(2)}, u32[]{:S(2)}) %collective-permute-start.20) | collective-permute-done | bytes 1048608 | tf_op jit(solution)/shard_map/ppermute | solution.py:192
  173.8 4.4 collective-permute-start.12
  178.3 18.0 %collective-permute-done.21.refs_21_ = f32[1,512,512]{2,1,0:T(8,128)S(1)} collective-permute-done((f32[1,512,512]{2,1,0:T(8,128)S(1)}, f32[1,512,512]{2,1,0:T(8,128)S(1)}, u32[]{:S(2)}, u32[]{:S(2)}) %collective-permute-start.21) | collective-permute-done | bytes 1048608 | tf_op jit(solution)/shard_map/ppermute | solution.py:192
  197.8 1.3 collective-permute-start.35
  199.1 1.3 collective-permute-start.36
  200.4 18.2 %collective-permute-done.12.refs_22_ = f32[1,512,512]{2,1,0:T(8,128)S(1)} collective-permute-done((f32[1,512,512]{2,1,0:T(8,128)S(1)}, f32[1,512,512]{2,1,0:T(8,128)S(1)}, u32[]{:S(2)}, u32[]{:S(2)}) %collective-permute-start.12) | collective-permute-done | bytes 1048608 | tf_op jit(solution)/shard_map/ppermute | solution.py:192
  218.6 1.3 collective-permute-start.37
  220.7 1.0 copy-done
  221.6 1.3 collective-permute-start.18
  222.9 46.5 %collective-permute-done.35.refs_36_ = f32[1,512,512]{2,1,0:T(8,128)S(1)} collective-permute-done((f32[1,512,512]{2,1,0:T(8,128)S(1)}, f32[1,512,512]{2,1,0:T(8,128)S(1)}, u32[]{:S(2)}, u32[]{:S(2)}) %collective-permute-start.35) | collective-permute-done | bytes 1048608 | tf_op jit(solution)/shard_map/ppermute | solution.py:192
  270.2 1.0 copy-done.2
  271.1 22.6 %collective-permute-done.36.refs_37_ = f32[1,512,512]{2,1,0:T(8,128)} collective-permute-done((f32[1,512,512]{2,1,0:T(8,128)S(1)}, f32[1,512,512]{2,1,0:T(8,128)}, u32[]{:S(2)}, u32[]{:S(2)}) %collective-permute-start.36) | collective-permute-done | bytes 1048608 | tf_op jit(solution)/shard_map/ppermute | solution.py:192
  294.4 20.0 %collective-permute-done.37.refs_38_ = f32[1,512,512]{2,1,0:T(8,128)} collective-permute-done((f32[1,512,512]{2,1,0:T(8,128)S(1)}, f32[1,512,512]{2,1,0:T(8,128)}, u32[]{:S(2)}, u32[]{:S(2)}) %collective-permute-start.37) | collective-permute-done | bytes 1048608 | tf_op jit(solution)/shard_map/ppermute | solution.py:192
  315.2 1.0 copy-done.6
  318.7 1.6 collective-permute-start.13
  321.3 1.3 collective-permute-start.38
  322.6 1.3 collective-permute-start.39
  324.8 80.8 %collective-permute-done.38.refs_39_ = f32[1,512,512]{2,1,0:T(8,128)S(1)} collective-permute-done((f32[1,512,512]{2,1,0:T(8,128)S(1)}, f32[1,512,512]{2,1,0:T(8,128)S(1)}, u32[]{:S(2)}, u32[]{:S(2)}) %collective-permute-start.38) | collective-permute-done | bytes 1048608 | tf_op jit(solution)/shard_map/ppermute | solution.py:192
  406.3 20.6 %collective-permute-done.39.refs_40_ = f32[1,512,512]{2,1,0:T(8,128)S(1)} collective-permute-done((f32[1,512,512]{2,1,0:T(8,128)S(1)}, f32[1,512,512]{2,1,0:T(8,128)S(1)}, u32[]{:S(2)}, u32[]{:S(2)}) %collective-permute-start.39) | collective-permute-done | bytes 1048608 | tf_op jit(solution)/shard_map/ppermute | solution.py:192
  426.9 1.9 collective-permute-start.40
  428.9 2.4 collective-permute-start.19
  431.3 1.9 collective-permute-start.41
  433.3 2.4 collective-permute-start.42
  436.7 1.3 collective-permute-start.15
  439.0 1.9 collective-permute-start.43
  441.0 2.4 collective-permute-start.44
  451.5 3.6 constant_dynamic-slice_fusion
  455.1 8.9 %collective-permute-done.15.refs_18_ = f32[1,512,512]{2,1,0:T(8,128)} collective-permute-done((f32[1,512,512]{2,1,0:T(8,128)}, f32[1,512,512]{2,1,0:T(8,128)}, u32[]{:S(2)}, u32[]{:S(2)}) %collective-permute-start.15) | collective-permute-done | bytes 1048608 | tf_op jit(solution)/shard_map/ppermute | solution.py:192
  464.0 1.5 collective-permute-start.2
  466.0 1.5 collective-permute-start
  468.1 1.3 collective-permute-start.4
  469.4 20.8 %collective-permute-done.2.refs_6_ = f32[1,512,512]{2,1,0:T(8,128)} collective-permute-done((f32[1,512,512]{2,1,0:T(8,128)S(1)}, f32[1,512,512]{2,1,0:T(8,128)}, u32[]{:S(2)}, u32[]{:S(2)}) %collective-permute-start.2) | collective-permute-done | bytes 1048608 | tf_op jit(solution)/shard_map/ppermute | solution.py:192
  490.1 1.3 collective-permute-start.5
  491.4 21.1 %collective-permute-done.3.refs_7_ = f32[1,512,512]{2,1,0:T(8,128)S(1)} collective-permute-done((f32[1,512,512]{2,1,0:T(8,128)S(1)}, f32[1,512,512]{2,1,0:T(8,128)S(1)}, u32[]{:S(2)}, u32[]{:S(2)}) %collective-permute-start.3) | collective-permute-done | bytes 1048608 | tf_op jit(solution)/shard_map/ppermute | solution.py:192
  512.5 1.3 collective-permute-start.6
  513.8 21.2 %collective-permute-done.refs_4_ = f32[1,512,512]{2,1,0:T(8,128)S(1)} collective-permute-done((f32[1,512,512]{2,1,0:T(8,128)}, f32[1,512,512]{2,1,0:T(8,128)S(1)}, u32[]{:S(2)}, u32[]{:S(2)}) %collective-permute-start) | collective-permute-done | bytes 1048608 | tf_op jit(solution)/shard_map/ppermute | solution.py:192
  535.0 1.3 collective-permute-start.7
  536.3 19.4 %collective-permute-done.1.refs_5_ = f32[1,512,512]{2,1,0:T(8,128)S(1)} collective-permute-done((f32[1,512,512]{2,1,0:T(8,128)S(1)}, f32[1,512,512]{2,1,0:T(8,128)S(1)}, u32[]{:S(2)}, u32[]{:S(2)}) %collective-permute-start.1) | collective-permute-done | bytes 1048608 | tf_op jit(solution)/shard_map/ppermute | solution.py:192
  555.6 4.4 collective-permute-start.10
  560.1 2.3 collective-permute-start.11
  562.4 2.3 collective-permute-start.8
  564.7 2.3 collective-permute-start.9
  568.2 1.7 collective-permute-start.14
  569.9 13.1 %collective-permute-done.10.refs_14_ = f32[1,512,512]{2,1,0:T(8,128)} collective-permute-done((f32[1,512,512]{2,1,0:T(8,128)}, f32[1,512,512]{2,1,0:T(8,128)}, u32[]{:S(2)}, u32[]{:S(2)}) %collective-permute-start.10) | collective-permute-done | bytes 1048608 | tf_op jit(solution)/shard_map/ppermute | solution.py:192
  582.9 1.9 collective-permute-start.16
  584.9 2.0 and_select_fusion.1
  586.9 18.5 %collective-permute-done.11.refs_15_ = f32[1,512,512]{2,1,0:T(8,128)} collective-permute-done((f32[1,512,512]{2,1,0:T(8,128)}, f32[1,512,512]{2,1,0:T(8,128)}, u32[]{:S(2)}, u32[]{:S(2)}) %collective-permute-start.11) | collective-permute-done | bytes 1048608 | tf_op jit(solution)/shard_map/ppermute | solution.py:192
  605.4 22.5 %collective-permute-done.8.refs_12_ = f32[1,512,512]{2,1,0:T(8,128)} collective-permute-done((f32[1,512,512]{2,1,0:T(8,128)}, f32[1,512,512]{2,1,0:T(8,128)}, u32[]{:S(2)}, u32[]{:S(2)}) %collective-permute-start.8) | collective-permute-done | bytes 1048608 | tf_op jit(solution)/shard_map/ppermute | solution.py:192
  627.9 19.8 %collective-permute-done.9.refs_13_ = f32[1,512,512]{2,1,0:T(8,128)} collective-permute-done((f32[1,512,512]{2,1,0:T(8,128)}, f32[1,512,512]{2,1,0:T(8,128)}, u32[]{:S(2)}, u32[]{:S(2)}) %collective-permute-start.9) | collective-permute-done | bytes 1048608 | tf_op jit(solution)/shard_map/ppermute | solution.py:192
  647.7 1.2 copy-done.1
  648.9 1.2 copy-done.3
  650.1 1.2 copy-done.5
  651.4 1.2 copy-done.7
  652.6 1.2 copy-done.9
  653.8 1.2 copy-done.11
  655.0 1.2 copy-done.14
  656.3 1.2 copy-done.16
  657.5 24.0 %shard_map.64.refs_20_ = f32[4,512,512]{2,1,0:T(8,128)} custom-call(s32[6,36]{1,0:T(8,128)S(1)} %stack.2.table, f32[1,512,512]{2,1,0:T(8,128)} %get-tuple-element.22.refs_0_, f32[1,512,512]{2,1,0:T(8,128)S(1)} %get-tuple-element.21.refs_1_, f32[1,512,512]{2,1,0:T(8,128)S(1)} %get-tuple-element.20.refs_2_, f32[1,512,512]{2,1,0:T(8,128)S(1)} %get-tuple-element.19.refs_3_, ...), custom_call_target="tpu_custom_call" | custom-call | flops 8053063680 | bytes 20971520 | tf_op jit(solution)/shard_map/pallas_call | solution.py:98
  681.6 7.9 %shard_map.65 = f32[4,512,512]{2,1,0:T(8,128)} custom-call(s32[6,36]{1,0:T(8,128)S(1)} %stack.2.table, f32[1,512,512]{2,1,0:T(8,128)} %get-tuple-element.22.refs_0_, f32[1,512,512]{2,1,0:T(8,128)S(1)} %get-tuple-element.21.refs_1_, f32[1,512,512]{2,1,0:T(8,128)S(1)} %get-tuple-element.20.refs_2_, f32[1,512,512]{2,1,0:T(8,128)S(1)} %get-tuple-element.19.refs_3_, ...), custom_call_target="tpu_custom_call" | custom-call | flops 8053063680 | bytes 20971520 | tf_op jit(solution)/shard_map/pallas_call | solution.py:98
  (126 shorter events, 19.1 us)
Async XLA Ops:
  6.8 431.2 %all-to-all-start = ((f32[8,520,512]{2,1,0:T(8,128)}), f32[8,520,512]{2,1,0:T(8,128)}, u32[]{:S(2)}, u32[]{:S(2)}) async-start(f32[8,520,512]{2,1,0:T(8,128)} %pack.1), calls=%async_computation | async-start | bytes 17039360 | tf_op jit(solution)/shard_map/all_to_all | solution.py:199
  15.3 158.6 %collective-permute-start.20 = (f32[1,512,512]{2,1,0:T(8,128)S(1)}, f32[1,512,512]{2,1,0:T(8,128)S(1)}, u32[]{:S(2)}, u32[]{:S(2)}) collective-permute-start(f32[1,512,512]{2,1,0:T(8,128)S(1)} %get-tuple-element.25), channel_id=1, source_target_pairs={{0,8},{4,12},{24,16},{28,20},{1,9},{5,13},{25,17},{29,21},{2,10},{... | collective-permute-start | bytes 3145736 | tf_op jit(solution)/shard_map/ppermute | solution.py:192
  19.3 177.0 %collective-permute-start.21 = (f32[1,512,512]{2,1,0:T(8,128)S(1)}, f32[1,512,512]{2,1,0:T(8,128)S(1)}, u32[]{:S(2)}, u32[]{:S(2)}) collective-permute-start(f32[1,512,512]{2,1,0:T(8,128)S(1)} %get-tuple-element.23), channel_id=1, source_target_pairs={{0,8},{4,12},{24,16},{28,20},{1,9},{5,13},{25,17},{29,21},{2,10},{... | collective-permute-start | bytes 3145736 | tf_op jit(solution)/shard_map/ppermute | solution.py:192
  20.6 176.4 %collective-permute-start.25 = (f32[1,512,512]{2,1,0:T(8,128)S(1)}, f32[1,512,512]{2,1,0:T(8,128)S(1)}, u32[]{:S(2)}, u32[]{:S(2)}) collective-permute-start(f32[1,512,512]{2,1,0:T(8,128)S(1)} %get-tuple-element.25), channel_id=1, source_target_pairs={{8,16},{12,20},{16,8},{20,12},{9,17},{13,21},{17,9},{21,13},{10,18... | collective-permute-start | bytes 3145736 | tf_op jit(solution)/shard_map/ppermute | solution.py:192
  21.4 176.4 %collective-permute-start.26 = (f32[1,512,512]{2,1,0:T(8,128)S(1)}, f32[1,512,512]{2,1,0:T(8,128)S(1)}, u32[]{:S(2)}, u32[]{:S(2)}) collective-permute-start(f32[1,512,512]{2,1,0:T(8,128)S(1)} %get-tuple-element.23), channel_id=1, source_target_pairs={{8,16},{12,20},{16,8},{20,12},{9,17},{13,21},{17,9},{21,13},{10,18... | collective-permute-start | bytes 3145736 | tf_op jit(solution)/shard_map/ppermute | solution.py:192
  22.1 177.0 %collective-permute-start.27 = (f32[1,512,512]{2,1,0:T(8,128)S(1)}, f32[1,512,512]{2,1,0:T(8,128)S(1)}, u32[]{:S(2)}, u32[]{:S(2)}) collective-permute-start(f32[1,512,512]{2,1,0:T(8,128)S(1)} %get-tuple-element.24), channel_id=1, source_target_pairs={{8,16},{12,20},{16,8},{20,12},{9,17},{13,21},{17,9},{21,13},{10,18... | collective-permute-start | bytes 3145736 | tf_op jit(solution)/shard_map/ppermute | solution.py:192
  173.8 44.8 %collective-permute-start.12 = (f32[1,512,512]{2,1,0:T(8,128)S(1)}, f32[1,512,512]{2,1,0:T(8,128)S(1)}, u32[]{:S(2)}, u32[]{:S(2)}) collective-permute-start(f32[1,512,512]{2,1,0:T(8,128)S(1)} %get-tuple-element.24), channel_id=1, source_target_pairs={{0,8},{4,12},{24,16},{28,20},{1,9},{5,13},{25,17},{29,21},{2,10},{... | collective-permute-start | bytes 3145736 | tf_op jit(solution)/shard_map/ppermute | solution.py:192
  196.3 23.6 %collective-permute-start.28 = (f32[1,512,512]{2,1,0:T(8,128)S(1)}, f32[1,512,512]{2,1,0:T(8,128)S(1)}, u32[]{:S(2)}, u32[]{:S(2)}) collective-permute-start(f32[1,512,512]{2,1,0:T(8,128)S(1)} %collective-permute-done.20.refs_20_), channel_id=1, source_target_pairs={{8,16},{12,20},{16,8},{20,12},{9,17},{13,21},{17,9},{21,13},{10,18... | collective-permute-start | bytes 3145736 | tf_op jit(solution)/shard_map/ppermute | solution.py:192
  197.1 126.9 %copy-start.17 = (f32[1,512,512]{2,1,0:T(8,128)}, f32[1,512,512]{2,1,0:T(8,128)S(1)}, u32[]{:S(2)}) copy-start(f32[1,512,512]{2,1,0:T(8,128)S(1)} %collective-permute-done.25.refs_26_) | copy-start | bytes 3145732
  197.1 24.6 %collective-permute-start.29 = (f32[1,512,512]{2,1,0:T(8,128)S(1)}, f32[1,512,512]{2,1,0:T(8,128)S(1)}, u32[]{:S(2)}, u32[]{:S(2)}) collective-permute-start(f32[1,512,512]{2,1,0:T(8,128)S(1)} %collective-permute-done.21.refs_21_), channel_id=1, source_target_pairs={{8,16},{12,20},{16,8},{20,12},{9,17},{13,21},{17,9},{21,13},{10,18... | collective-permute-start | bytes 3145736 | tf_op jit(solution)/shard_map/ppermute | solution.py:192
  197.8 126.9 %copy-start.18 = (f32[1,512,512]{2,1,0:T(8,128)}, f32[1,512,512]{2,1,0:T(8,128)S(1)}, u32[]{:S(2)}) copy-start(f32[1,512,512]{2,1,0:T(8,128)S(1)} %collective-permute-done.26.refs_27_) | copy-start | bytes 3145732
  197.8 71.6 %collective-permute-start.35 = (f32[1,512,512]{2,1,0:T(8,128)S(1)}, f32[1,512,512]{2,1,0:T(8,128)S(1)}, u32[]{:S(2)}, u32[]{:S(2)}) collective-permute-start(f32[1,512,512]{2,1,0:T(8,128)S(1)} %collective-permute-done.25.refs_26_), channel_id=1, source_target_pairs={{8,0},{12,4},{16,24},{20,28},{9,1},{13,5},{17,25},{21,29},{10,2},{... | collective-permute-start | bytes 3145736 | tf_op jit(solution)/shard_map/ppermute | solution.py:192
  199.1 206.5 %copy-start.19 = (f32[1,512,512]{2,1,0:T(8,128)}, f32[1,512,512]{2,1,0:T(8,128)S(1)}, u32[]{:S(2)}) copy-start(f32[1,512,512]{2,1,0:T(8,128)S(1)} %collective-permute-done.27.refs_28_) | copy-start | bytes 3145732
  199.1 94.6 %collective-permute-start.36 = (f32[1,512,512]{2,1,0:T(8,128)S(1)}, f32[1,512,512]{2,1,0:T(8,128)}, u32[]{:S(2)}, u32[]{:S(2)}) collective-permute-start(f32[1,512,512]{2,1,0:T(8,128)S(1)} %collective-permute-done.26.refs_27_), channel_id=1, source_target_pairs={{8,0},{12,4},{16,24},{20,28},{9,1},{13,5},{17,25},{21,29},{10,2},{... | collective-permute-start | bytes 3145736 | tf_op jit(solution)/shard_map/ppermute | solution.py:192
  218.6 95.9 %collective-permute-start.37 = (f32[1,512,512]{2,1,0:T(8,128)S(1)}, f32[1,512,512]{2,1,0:T(8,128)}, u32[]{:S(2)}, u32[]{:S(2)}) collective-permute-start(f32[1,512,512]{2,1,0:T(8,128)S(1)} %collective-permute-done.27.refs_28_), channel_id=1, source_target_pairs={{8,0},{12,4},{16,24},{20,28},{9,1},{13,5},{17,25},{21,29},{10,2},{... | collective-permute-start | bytes 3145736 | tf_op jit(solution)/shard_map/ppermute | solution.py:192
  219.9 186.4 %copy-start.20 = (f32[1,512,512]{2,1,0:T(8,128)}, f32[1,512,512]{2,1,0:T(8,128)S(1)}, u32[]{:S(2)}) copy-start(f32[1,512,512]{2,1,0:T(8,128)S(1)} %collective-permute-done.28.refs_29_) | copy-start | bytes 3145732
  219.9 95.3 %collective-permute-start.22 = (f32[1,512,512]{2,1,0:T(8,128)S(1)}, f32[1,512,512]{2,1,0:T(8,128)S(1)}, u32[]{:S(2)}, u32[]{:S(2)}) collective-permute-start(f32[1,512,512]{2,1,0:T(8,128)S(1)} %collective-permute-done.20.refs_20_), channel_id=1, source_target_pairs={{8,12},{12,8},{16,20},{20,16},{9,13},{13,9},{17,21},{21,17},{10,14... | collective-permute-start | bytes 3145736 | tf_op jit(solution)/shard_map/ppermute | solution.py:192
  221.6 209.6 %copy-start.21 = (f32[1,512,512]{2,1,0:T(8,128)}, f32[1,512,512]{2,1,0:T(8,128)S(1)}, u32[]{:S(2)}) copy-start(f32[1,512,512]{2,1,0:T(8,128)S(1)} %collective-permute-done.29.refs_30_) | copy-start | bytes 3145732
  221.6 207.2 %collective-permute-start.18 = (f32[3,512,512]{2,1,0:T(8,128)}, f32[3,512,512]{2,1,0:T(8,128)}, u32[]{:S(2)}, u32[]{:S(2)}) collective-permute-start(f32[3,512,512]{2,1,0:T(8,128)} %bitcast.17.refs_16_), channel_id=1, source_target_pairs={{8,0},{12,4},{16,24},{20,28},{9,1},{13,5},{17,25},{21,29},{10,2},{... | collective-permute-start | bytes 9437192 | tf_op jit(solution)/shard_map/ppermute | solution.py:192
  269.4 163.8 %copy-start.22 = (f32[1,512,512]{2,1,0:T(8,128)}, f32[1,512,512]{2,1,0:T(8,128)S(1)}, u32[]{:S(2)}) copy-start(f32[1,512,512]{2,1,0:T(8,128)S(1)} %collective-permute-done.35.refs_36_) | copy-start | bytes 3145732
  269.4 47.5 %collective-permute-start.23 = (f32[1,512,512]{2,1,0:T(8,128)S(1)}, f32[1,512,512]{2,1,0:T(8,128)S(1)}, u32[]{:S(2)}, u32[]{:S(2)}) collective-permute-start(f32[1,512,512]{2,1,0:T(8,128)S(1)} %collective-permute-done.21.refs_21_), channel_id=1, source_target_pairs={{8,12},{12,8},{16,20},{20,16},{9,13},{13,9},{17,21},{21,17},{10,14... | collective-permute-start | bytes 3145736 | tf_op jit(solution)/shard_map/ppermute | solution.py:192
  293.7 24.9 %collective-permute-start.24 = (f32[1,512,512]{2,1,0:T(8,128)S(1)}, f32[1,512,512]{2,1,0:T(8,128)S(1)}, u32[]{:S(2)}, u32[]{:S(2)}) collective-permute-start(f32[1,512,512]{2,1,0:T(8,128)S(1)} %collective-permute-done.12.refs_22_), channel_id=1, source_target_pairs={{8,12},{12,8},{16,20},{20,16},{9,13},{13,9},{17,21},{21,17},{10,14... | collective-permute-start | bytes 3145736 | tf_op jit(solution)/shard_map/ppermute | solution.py:192
  314.5 6.8 collective-permute-start.30
  316.2 6.4 collective-permute-start.31
  317.9 6.0 collective-permute-start.32
  318.6 117.0 %copy-start.23 = (f32[1,512,512]{2,1,0:T(8,128)}, f32[1,512,512]{2,1,0:T(8,128)S(1)}, u32[]{:S(2)}) copy-start(f32[1,512,512]{2,1,0:T(8,128)S(1)} %collective-permute-done.24.refs_25_) | copy-start | bytes 3145732
  318.7 5.3 collective-permute-start.13
  321.3 114.4 %copy-start.24 = (f32[1,512,512]{2,1,0:T(8,128)}, f32[1,512,512]{2,1,0:T(8,128)S(1)}, u32[]{:S(2)}) copy-start(f32[1,512,512]{2,1,0:T(8,128)S(1)} %collective-permute-done.30.refs_31_) | copy-start | bytes 3145732
  321.3 84.3 %collective-permute-start.38 = (f32[1,512,512]{2,1,0:T(8,128)S(1)}, f32[1,512,512]{2,1,0:T(8,128)S(1)}, u32[]{:S(2)}, u32[]{:S(2)}) collective-permute-start(f32[1,512,512]{2,1,0:T(8,128)S(1)} %collective-permute-done.28.refs_29_), channel_id=1, source_target_pairs={{8,0},{12,4},{16,24},{20,28},{9,1},{13,5},{17,25},{21,29},{10,2},{... | collective-permute-start | bytes 3145736 | tf_op jit(solution)/shard_map/ppermute | solution.py:192
  322.6 128.2 %copy-start.25 = (f32[1,512,512]{2,1,0:T(8,128)}, f32[1,512,512]{2,1,0:T(8,128)S(1)}, u32[]{:S(2)}) copy-start(f32[1,512,512]{2,1,0:T(8,128)S(1)} %collective-permute-done.31.refs_32_) | copy-start | bytes 3145732
  322.6 104.3 %collective-permute-start.39 = (f32[1,512,512]{2,1,0:T(8,128)S(1)}, f32[1,512,512]{2,1,0:T(8,128)S(1)}, u32[]{:S(2)}, u32[]{:S(2)}) collective-permute-start(f32[1,512,512]{2,1,0:T(8,128)S(1)} %collective-permute-done.29.refs_30_), channel_id=1, source_target_pairs={{8,0},{12,4},{16,24},{20,28},{9,1},{13,5},{17,25},{21,29},{10,2},{... | collective-permute-start | bytes 3145736 | tf_op jit(solution)/shard_map/ppermute | solution.py:192
  323.9 126.8 %copy-start.26 = (f32[1,512,512]{2,1,0:T(8,128)}, f32[1,512,512]{2,1,0:T(8,128)S(1)}, u32[]{:S(2)}) copy-start(f32[1,512,512]{2,1,0:T(8,128)S(1)} %collective-permute-done.32.refs_33_) | copy-start | bytes 3145732
  323.9 141.6 %collective-permute-start.17 = (f32[3,512,512]{2,1,0:T(8,128)}, f32[3,512,512]{2,1,0:T(8,128)}, u32[]{:S(2)}, u32[]{:S(2)}) collective-permute-start(f32[3,512,512]{2,1,0:T(8,128)} %bitcast.17.refs_16_), channel_id=1, source_target_pairs={{0,4},{4,0},{8,12},{12,8},{16,20},{20,16},{24,28},{28,24},{1,5},{5... | collective-permute-start | bytes 9437192 | tf_op jit(solution)/shard_map/ppermute | solution.py:192
  324.0 107.3 %collective-permute-start.33 = (f32[1,512,512]{2,1,0:T(8,128)S(1)}, f32[1,512,512]{2,1,0:T(8,128)S(1)}, u32[]{:S(2)}, u32[]{:S(2)}) collective-permute-start(f32[1,512,512]{2,1,0:T(8,128)S(1)} %collective-permute-done.28.refs_29_), channel_id=1, source_target_pairs={{8,12},{12,8},{16,20},{20,16},{9,13},{13,9},{17,21},{21,17},{10,14... | collective-permute-start | bytes 3145736 | tf_op jit(solution)/shard_map/ppermute | solution.py:192
  405.6 30.1 %copy-start.27 = (f32[1,512,512]{2,1,0:T(8,128)}, f32[1,512,512]{2,1,0:T(8,128)S(1)}, u32[]{:S(2)}) copy-start(f32[1,512,512]{2,1,0:T(8,128)S(1)} %collective-permute-done.38.refs_39_) | copy-start | bytes 3145732
  405.6 27.6 %collective-permute-start.34 = (f32[1,512,512]{2,1,0:T(8,128)S(1)}, f32[1,512,512]{2,1,0:T(8,128)S(1)}, u32[]{:S(2)}, u32[]{:S(2)}) collective-permute-start(f32[1,512,512]{2,1,0:T(8,128)S(1)} %collective-permute-done.29.refs_30_), channel_id=1, source_target_pairs={{8,12},{12,8},{16,20},{20,16},{9,13},{13,9},{17,21},{21,17},{10,14... | collective-permute-start | bytes 3145736 | tf_op jit(solution)/shard_map/ppermute | solution.py:192
  426.9 8.8 %collective-permute-start.40 = (f32[1,512,512]{2,1,0:T(8,128)S(1)}, f32[1,512,512]{2,1,0:T(8,128)S(1)}, u32[]{:S(2)}, u32[]{:S(2)}) collective-permute-start(f32[1,512,512]{2,1,0:T(8,128)S(1)} %collective-permute-done.35.refs_36_), channel_id=1, source_target_pairs={{0,4},{4,0},{24,28},{28,24},{1,5},{5,1},{25,29},{29,25},{2,6},{6,2... | collective-permute-start | bytes 3145736 | tf_op jit(solution)/shard_map/ppermute | solution.py:192
  428.9 39.2 %collective-permute-start.19 = (f32[3,512,512]{2,1,0:T(8,128)}, f32[3,512,512]{2,1,0:T(8,128)}, u32[]{:S(2)}, u32[]{:S(2)}) collective-permute-start(f32[3,512,512]{2,1,0:T(8,128)} %collective-permute-done.18.refs_18_), channel_id=1, source_target_pairs={{0,4},{4,0},{24,28},{28,24},{1,5},{5,1},{25,29},{29,25},{2,6},{6,2... | collective-permute-start | bytes 9437192 | tf_op jit(solution)/shard_map/ppermute | solution.py:192
  431.3 7.7 %collective-permute-start.41 = (f32[1,512,512]{2,1,0:T(8,128)}, f32[1,512,512]{2,1,0:T(8,128)}, u32[]{:S(2)}, u32[]{:S(2)}) collective-permute-start(f32[1,512,512]{2,1,0:T(8,128)} %collective-permute-done.36.refs_37_), channel_id=1, source_target_pairs={{0,4},{4,0},{24,28},{28,24},{1,5},{5,1},{25,29},{29,25},{2,6},{6,2... | collective-permute-start | bytes 3145736 | tf_op jit(solution)/shard_map/ppermute | solution.py:192
  433.3 7.7 %collective-permute-start.42 = (f32[1,512,512]{2,1,0:T(8,128)}, f32[1,512,512]{2,1,0:T(8,128)}, u32[]{:S(2)}, u32[]{:S(2)}) collective-permute-start(f32[1,512,512]{2,1,0:T(8,128)} %collective-permute-done.37.refs_38_), channel_id=1, source_target_pairs={{0,4},{4,0},{24,28},{28,24},{1,5},{5,1},{25,29},{29,25},{2,6},{6,2... | collective-permute-start | bytes 3145736 | tf_op jit(solution)/shard_map/ppermute | solution.py:192
  436.7 27.3 %collective-permute-start.15 = (f32[1,512,512]{2,1,0:T(8,128)}, f32[1,512,512]{2,1,0:T(8,128)}, u32[]{:S(2)}, u32[]{:S(2)}) collective-permute-start(f32[1,512,512]{2,1,0:T(8,128)} %collective-permute-done.13.refs_16_), channel_id=1, source_target_pairs={{8,0},{12,4},{16,24},{20,28},{9,1},{13,5},{17,25},{21,29},{10,2},{... | collective-permute-start | bytes 3145736 | tf_op jit(solution)/shard_map/ppermute | solution.py:192
  439.0 27.0 %collective-permute-start.43 = (f32[1,512,512]{2,1,0:T(8,128)}, f32[1,512,512]{2,1,0:T(8,128)}, u32[]{:S(2)}, u32[]{:S(2)}) collective-permute-start(f32[1,512,512]{2,1,0:T(8,128)} %copy-done.27), channel_id=1, source_target_pairs={{0,4},{4,0},{24,28},{28,24},{1,5},{5,1},{25,29},{29,25},{2,6},{6,2... | collective-permute-start | bytes 3145736 | tf_op jit(solution)/shard_map/ppermute | solution.py:192
  441.0 26.6 %collective-permute-start.44 = (f32[1,512,512]{2,1,0:T(8,128)}, f32[1,512,512]{2,1,0:T(8,128)}, u32[]{:S(2)}, u32[]{:S(2)}) collective-permute-start(f32[1,512,512]{2,1,0:T(8,128)} %copy-done.28), channel_id=1, source_target_pairs={{0,4},{4,0},{24,28},{28,24},{1,5},{5,1},{25,29},{29,25},{2,6},{6,2... | collective-permute-start | bytes 3145736 | tf_op jit(solution)/shard_map/ppermute | solution.py:192
  451.4 108.7 %copy-start.33 = (s32[1,1,3,12,3]{3,1,4,2,0:T(1,128)S(1)}, s32[1,1,3,12,3]{3,1,4,2,0:T(1,128)}, u32[]{:S(2)}) copy-start(s32[1,1,3,12,3]{3,1,4,2,0:T(1,128)} %param.12) | copy-start | bytes 1300
  451.4 115.7 %copy-start.32 = (s32[1,1,3]{2,1,0:T(1,128)S(1)}, s32[1,1,3]{2,1,0:T(1,128)}, u32[]{:S(2)}) copy-start(s32[1,1,3]{2,1,0:T(1,128)} %param.13) | copy-start | bytes 40
  451.4 133.4 %copy-start.34 = (pred[36]{0:T(512)(128)(4,1)S(1)}, pred[36]{0:T(512)(128)(4,1)}, u32[]{:S(2)}) copy-start(pred[36]{0:T(512)(128)(4,1)} %constant.228) | copy-start | bytes 112
  451.4 133.4 %copy-start.35 = (pred[36]{0:T(512)(128)(4,1)S(1)}, pred[36]{0:T(512)(128)(4,1)}, u32[]{:S(2)}) copy-start(pred[36]{0:T(512)(128)(4,1)} %constant.229) | copy-start | bytes 112
  464.0 26.1 %collective-permute-start.2 = (f32[1,512,512]{2,1,0:T(8,128)S(1)}, f32[1,512,512]{2,1,0:T(8,128)}, u32[]{:S(2)}, u32[]{:S(2)}) collective-permute-start(f32[1,512,512]{2,1,0:T(8,128)S(1)} %get-tuple-element.20.refs_2_), channel_id=1, source_target_pairs={{2,0},{3,1},{0,2},{1,3},{6,4},{7,5},{4,6},{5,7},{10,8},{11,9},{8,1... | collective-permute-start | bytes 3145736 | tf_op jit(solution)/shard_map/ppermute | solution.py:192
  465.5 47.0 %collective-permute-start.3 = (f32[1,512,512]{2,1,0:T(8,128)S(1)}, f32[1,512,512]{2,1,0:T(8,128)S(1)}, u32[]{:S(2)}, u32[]{:S(2)}) collective-permute-start(f32[1,512,512]{2,1,0:T(8,128)S(1)} %get-tuple-element.19.refs_3_), channel_id=1, source_target_pairs={{2,0},{3,1},{0,2},{1,3},{6,4},{7,5},{4,6},{5,7},{10,8},{11,9},{8,1... | collective-permute-start | bytes 3145736 | tf_op jit(solution)/shard_map/ppermute | solution.py:192
  466.0 68.9 %collective-permute-start = (f32[1,512,512]{2,1,0:T(8,128)}, f32[1,512,512]{2,1,0:T(8,128)S(1)}, u32[]{:S(2)}, u32[]{:S(2)}) collective-permute-start(f32[1,512,512]{2,1,0:T(8,128)} %get-tuple-element.22.refs_0_), channel_id=1, source_target_pairs={{2,0},{3,1},{0,2},{1,3},{6,4},{7,5},{4,6},{5,7},{10,8},{11,9},{8,1... | collective-permute-start | bytes 3145736 | tf_op jit(solution)/shard_map/ppermute | solution.py:192
  467.6 88.1 %collective-permute-start.1 = (f32[1,512,512]{2,1,0:T(8,128)S(1)}, f32[1,512,512]{2,1,0:T(8,128)S(1)}, u32[]{:S(2)}, u32[]{:S(2)}) collective-permute-start(f32[1,512,512]{2,1,0:T(8,128)S(1)} %get-tuple-element.21.refs_1_), channel_id=1, source_target_pairs={{2,0},{3,1},{0,2},{1,3},{6,4},{7,5},{4,6},{5,7},{10,8},{11,9},{8,1... | collective-permute-start | bytes 3145736 | tf_op jit(solution)/shard_map/ppermute | solution.py:192
  468.1 92.1 %collective-permute-start.4 = (f32[1,512,512]{2,1,0:T(8,128)}, f32[1,512,512]{2,1,0:T(8,128)}, u32[]{:S(2)}, u32[]{:S(2)}) collective-permute-start(f32[1,512,512]{2,1,0:T(8,128)} %get-tuple-element.22.refs_0_), channel_id=1, source_target_pairs={{1,0},{3,2},{5,4},{7,6},{9,8},{11,10},{13,12},{15,14},{17,16},{19,... | collective-permute-start | bytes 3145736 | tf_op jit(solution)/shard_map/ppermute | solution.py:192
  490.1 72.3 %collective-permute-start.5 = (f32[1,512,512]{2,1,0:T(8,128)S(1)}, f32[1,512,512]{2,1,0:T(8,128)}, u32[]{:S(2)}, u32[]{:S(2)}) collective-permute-start(f32[1,512,512]{2,1,0:T(8,128)S(1)} %get-tuple-element.21.refs_1_), channel_id=1, source_target_pairs={{1,0},{3,2},{5,4},{7,6},{9,8},{11,10},{13,12},{15,14},{17,16},{19,... | collective-permute-start | bytes 3145736 | tf_op jit(solution)/shard_map/ppermute | solution.py:192
  512.5 43.1 %copy-start.10 = (f32[1,512,512]{2,1,0:T(8,128)}, f32[1,512,512]{2,1,0:T(8,128)S(1)}, u32[]{:S(2)}) copy-start(f32[1,512,512]{2,1,0:T(8,128)S(1)} %collective-permute-done.3.refs_7_) | copy-start | bytes 3145732
  512.5 52.2 %collective-permute-start.6 = (f32[1,512,512]{2,1,0:T(8,128)S(1)}, f32[1,512,512]{2,1,0:T(8,128)}, u32[]{:S(2)}, u32[]{:S(2)}) collective-permute-start(f32[1,512,512]{2,1,0:T(8,128)S(1)} %get-tuple-element.20.refs_2_), channel_id=1, source_target_pairs={{1,0},{3,2},{5,4},{7,6},{9,8},{11,10},{13,12},{15,14},{17,16},{19,... | collective-permute-start | bytes 3145736 | tf_op jit(solution)/shard_map/ppermute | solution.py:192
  535.0 25.1 %copy-start.13 = (f32[1,512,512]{2,1,0:T(8,128)}, f32[1,512,512]{2,1,0:T(8,128)S(1)}, u32[]{:S(2)}) copy-start(f32[1,512,512]{2,1,0:T(8,128)S(1)} %collective-permute-done.refs_4_) | copy-start | bytes 3145732
  535.0 33.2 %collective-permute-start.7 = (f32[1,512,512]{2,1,0:T(8,128)S(1)}, f32[1,512,512]{2,1,0:T(8,128)}, u32[]{:S(2)}, u32[]{:S(2)}) collective-permute-start(f32[1,512,512]{2,1,0:T(8,128)S(1)} %get-tuple-element.19.refs_3_), channel_id=1, source_target_pairs={{1,0},{3,2},{5,4},{7,6},{9,8},{11,10},{13,12},{15,14},{17,16},{19,... | collective-permute-start | bytes 3145736 | tf_op jit(solution)/shard_map/ppermute | solution.py:192
  555.6 27.3 %collective-permute-start.10 = (f32[1,512,512]{2,1,0:T(8,128)}, f32[1,512,512]{2,1,0:T(8,128)}, u32[]{:S(2)}, u32[]{:S(2)}) collective-permute-start(f32[1,512,512]{2,1,0:T(8,128)} %collective-permute-done.2.refs_6_), channel_id=1, source_target_pairs={{0,1},{2,3},{4,5},{6,7},{8,9},{10,11},{12,13},{14,15},{16,17},{18,... | collective-permute-start | bytes 3145736 | tf_op jit(solution)/shard_map/ppermute | solution.py:192
  560.1 45.2 %collective-permute-start.11 = (f32[1,512,512]{2,1,0:T(8,128)}, f32[1,512,512]{2,1,0:T(8,128)}, u32[]{:S(2)}, u32[]{:S(2)}) collective-permute-start(f32[1,512,512]{2,1,0:T(8,128)} %copy-done.10), channel_id=1, source_target_pairs={{0,1},{2,3},{4,5},{6,7},{8,9},{10,11},{12,13},{14,15},{16,17},{18,... | collective-permute-start | bytes 3145736 | tf_op jit(solution)/shard_map/ppermute | solution.py:192
  562.4 65.4 %collective-permute-start.8 = (f32[1,512,512]{2,1,0:T(8,128)}, f32[1,512,512]{2,1,0:T(8,128)}, u32[]{:S(2)}, u32[]{:S(2)}) collective-permute-start(f32[1,512,512]{2,1,0:T(8,128)} %copy-done.13), channel_id=1, source_target_pairs={{0,1},{2,3},{4,5},{6,7},{8,9},{10,11},{12,13},{14,15},{16,17},{18,... | collective-permute-start | bytes 3145736 | tf_op jit(solution)/shard_map/ppermute | solution.py:192
  564.7 83.0 %collective-permute-start.9 = (f32[1,512,512]{2,1,0:T(8,128)}, f32[1,512,512]{2,1,0:T(8,128)}, u32[]{:S(2)}, u32[]{:S(2)}) collective-permute-start(f32[1,512,512]{2,1,0:T(8,128)} %copy-done.15), channel_id=1, source_target_pairs={{0,1},{2,3},{4,5},{6,7},{8,9},{10,11},{12,13},{14,15},{16,17},{18,... | collective-permute-start | bytes 3145736 | tf_op jit(solution)/shard_map/ppermute | solution.py:192
  568.2 113.3 %collective-permute-start.14 = (f32[1,512,512]{2,1,0:T(8,128)}, f32[1,512,512]{2,1,0:T(8,128)}, u32[]{:S(2)}, u32[]{:S(2)}) collective-permute-start(f32[1,512,512]{2,1,0:T(8,128)} %collective-permute-done.13.refs_16_), channel_id=1, source_target_pairs={{8,12},{12,8},{16,20},{20,16},{9,13},{13,9},{17,21},{21,17},{10,14... | collective-permute-start | bytes 3145736 | tf_op jit(solution)/shard_map/ppermute | solution.py:192
  582.9 98.6 %collective-permute-start.16 = (f32[1,512,512]{2,1,0:T(8,128)}, f32[1,512,512]{2,1,0:T(8,128)}, u32[]{:S(2)}, u32[]{:S(2)}) collective-permute-start(f32[1,512,512]{2,1,0:T(8,128)} %collective-permute-done.15.refs_18_), channel_id=1, source_target_pairs={{0,4},{4,0},{24,28},{28,24},{1,5},{5,1},{25,29},{29,25},{2,6},{6,2... | collective-permute-start | bytes 3145736 | tf_op jit(solution)/shard_map/ppermute | solution.py:192
  657.5 24.1 %copy-start.12 = (f32[1,512,512]{2,1,0:T(8,128)S(1)}, f32[1,512,512]{2,1,0:T(8,128)}, u32[]{:S(2)}) copy-start(f32[1,512,512]{2,1,0:T(8,128)} %copy-done.10) | copy-start | bytes 3145732
  (18 other events, 50.9 us)
where the time goes:
time: 697 us; the launch traced here: 690 us
  waiting for transfers between devices  543 us (78%)
  starting transfers between devices  73.2 us (11%)
  Pallas kernels  36 us (5%)
  local copies, waits for them, and re-layouts  25.9 us (4%)
  between operations  8.25 us (1%)
    ppermute x45, waiting for transfers between devices, move(): return lax.ppermute(block, axis, pairs)  543 us
    ppermute x45, starting transfers between devices, move(): return lax.ppermute(block, axis, pairs)  66.8 us
    pallas_call x2, Pallas kernels, run_pairs(): pl.pallas_call(functools.partial(pairs_kernel, phase, n_left, n_right, fr...  32 us
    unnamed x75, local copies, waits for them, and re-layouts  17.3 us
  transfers between devices with their start and end apart: 46, of which 17 were waited for; matrix products, arithmetic and copies ran while one was open for 2% of the time, Pallas kernels for 3%

commit v1 on v0

--- a/solution.py
+++ b/solution.py
@@ -10,7 +10,6 @@
 
 OUT = 4
 STOPS = 3
-LAST = 1
 NOTE = 8
 CORES = 2
 
@@ -37,12 +36,11 @@
     lefts = refs[:n_left]
     rights = refs[n_left:n_left + n_right]
     rest = refs[n_left + n_right:]
-    if fresh:
-        out, todo, lbuf, rbuf, lsem, rsem = rest
-        out[...] = jnp.zeros_like(out)
-    else:
-        before, out, todo, lbuf, rbuf, lsem, rsem = rest
-        out[...] = before[...]
+    before, rest = (None, rest) if fresh else (rest[0], rest[1:])
+    out, todo, used, acc, lbuf, rbuf, lsem, rsem, asem = rest
+    slots = acc.shape[0]
+    for o in range(slots):
+        used[o] = jnp.int32(1 if fresh else 0)
 
     def pick(p, count):
         mine = table[5, p] == phase
@@ -50,6 +48,7 @@
         @pl.when(mine)
         def _():
             todo[count] = p
+            used[table[4, p]] = jnp.int32(1)
 
         return count + mine.astype(jnp.int32)
 
@@ -60,7 +59,7 @@
         for k, ref in enumerate(lefts):
             @pl.when(table[0, p] == k)
             def _(ref=ref):
-                pltpu.make_async_copy(ref.at[table[1, p]], lbuf.at[slot], lsem.at[slot]).start()
+                pltpu.make_async_copy(ref.at[0], lbuf.at[slot], lsem.at[slot]).start()
         for k, ref in enumerate(rights):
             @pl.when(table[2, p] == k)
             def _(ref=ref):
@@ -70,6 +69,18 @@
     def _():
         fetch(0, 0)
 
+    if fresh:
+        acc[...] = jnp.zeros_like(acc)
+    else:
+        for o in range(slots):
+            @pl.when(used[o] == 1)
+            def _(o=o):
+                pltpu.make_async_copy(before.at[o], acc.at[o], asem.at[o]).start()
+        for o in range(slots):
+            @pl.when(used[o] == 1)
+            def _(o=o):
+                pltpu.make_async_copy(before.at[o], acc.at[o], asem.at[o]).wait()
+
     def step(position, carry):
         slot = lax.rem(position, 2)
 
@@ -80,39 +91,49 @@
         pltpu.make_async_copy(lefts[0].at[0], lbuf.at[slot], lsem.at[slot]).wait()
         pltpu.make_async_copy(rights[0].at[0], rbuf.at[slot], rsem.at[slot]).wait()
         o = table[4, todo[position]]
-        out[o] += product(lbuf[slot], rbuf[slot])
+        acc[o] += product(lbuf[slot], rbuf[slot])
         return carry
 
     lax.fori_loop(0, count, step, 0)
+    for o in range(slots):
+        @pl.when(used[o] == 1)
+        def _(o=o):
+            pltpu.make_async_copy(acc.at[o], out.at[o], asem.at[o]).start()
+    for o in range(slots):
+        @pl.when(used[o] == 1)
+        def _(o=o):
+            pltpu.make_async_copy(acc.at[o], out.at[o], asem.at[o]).wait()
 
 
 def run_pairs(phase, table, lefts, rights, before, out_shape):
     n_left, n_right = len(lefts), len(rights)
-    width = out_shape[-1]
-    any_spec = pl.BlockSpec(memory_space=pl.ANY)
-    whole = pl.BlockSpec(memory_space=pltpu.VMEM)
+    slots, width = out_shape[0], out_shape[-1]
     fresh = before is None
     ins = list(lefts) + list(rights) + ([] if fresh else [before])
-    specs = [any_spec] * (n_left + n_right) + ([] if fresh else [whole])
-    work = 10 * width ** 3
+    any_spec = pl.BlockSpec(memory_space=pl.ANY)
+    block = 4 * width * width
     return pl.pallas_call(
         functools.partial(pairs_kernel, phase, n_left, n_right, fresh),
         out_shape=jax.ShapeDtypeStruct(out_shape, jnp.float32),
         grid_spec=pltpu.PrefetchScalarGridSpec(
             num_scalar_prefetch=1,
             grid=(),
-            in_specs=specs,
-            out_specs=whole,
+            in_specs=[any_spec] * len(ins),
+            out_specs=any_spec,
             scratch_shapes=[
                 pltpu.SMEM((table.shape[1],), jnp.int32),
+                pltpu.SMEM((slots,), jnp.int32),
+                pltpu.VMEM(out_shape, jnp.float32),
                 pltpu.VMEM((2, width, width), jnp.float32),
                 pltpu.VMEM((2, width, width), jnp.float32),
                 pltpu.SemaphoreType.DMA((2,)),
                 pltpu.SemaphoreType.DMA((2,)),
+                pltpu.SemaphoreType.DMA((slots,)),
             ],
         ),
+        input_output_aliases={} if fresh else {len(ins): 0},
         compiler_params=pltpu.CompilerParams(vmem_limit_bytes=32 << 20),
-        cost_estimate=pl.CostEstimate(flops=6 * work, bytes_accessed=20 * width * width * 4, transcendentals=0),
+        cost_estimate=pl.CostEstimate(flops=60 * width ** 3, bytes_accessed=20 * block, transcendentals=0),
     )(table, *ins)
 
 
@@ -251,21 +272,24 @@
     beside_ref = jnp.where(i_am_inner, 4 + crossed * half_count + q, 2 + crossed)
     right_ref = jnp.where(same, crossed, jnp.where(paired, beside_ref, far_ref))
     right_pos = jnp.where(jnp.logical_and(paired, right_ref < 4), q, 0)
-    cut = n_far - LAST
-    late = jnp.logical_and(jnp.logical_not(paired), far_index >= cut)
-    phase = jnp.where(live, late.astype(jnp.int32), -1)
+    cuts = (half_count, n_far - 1)
+    is_far = jnp.logical_not(paired)
     far_group, far_place = (right_ref - near_refs) // n_far, (right_ref - near_refs) % n_far
-    early_ref = jnp.where(right_ref < near_refs, right_ref, near_refs + far_group * cut + far_place)
-    late_ref = far_group * LAST + far_place - cut
-    table = jnp.stack([left_ref, left_pos, jnp.where(late, late_ref, early_ref), right_pos, o, phase], axis=0)
+    first = jnp.logical_and(stop != 1, jnp.logical_or(paired, far_index < cuts[0]))
+    late = jnp.logical_and(is_far, far_index >= cuts[1])
+    phase = jnp.where(live, jnp.where(late, 2, jnp.where(first, 0, 1)), -1)
+    near_or = lambda cut: jnp.where(is_far, near_refs + far_group * cut + far_place, right_ref)
+    last_ref = far_group * (n_far - cuts[1]) + far_place - cuts[1]
+    right_ref = jnp.where(late, last_ref, jnp.where(first, near_or(cuts[0]), near_or(cuts[1])))
+    table = jnp.stack([left_ref, left_pos, right_ref, right_pos, o, phase], axis=0)
 
     lefts = tile + after_two + after_one_even + after_one_odd
+    near = [ham, own_x, beside_out, beside_out_x] + beside_in + beside_in_x
     far = [far_mid, far_mid_x, far_out, far_out_x]
-    early_rights = [ham, own_x, beside_out, beside_out_x] + beside_in + beside_in_x + [r for g in far for r in g[:cut]]
-    late_rights = [r for g in far for r in g[cut:]]
     shape = (OUT, width, width)
-    result = run_pairs(0, table, lefts, early_rights, None, shape)
-    result = run_pairs(1, table, lefts, late_rights, result, shape)
+    result = run_pairs(0, table, tile + after_two, near + [r for g in far for r in g[:cuts[0]]], None, shape)
+    result = run_pairs(1, table, lefts, near + [r for g in far for r in g[:cuts[1]]], result, shape)
+    result = run_pairs(2, table, lefts, [r for g in far for r in g[cuts[1]:]], result, shape)
     return result[None, None]
 
 

time: 697 us -> 681 us (0.977)
  waiting for transfers between devices: 543 us -> 312 us
  starting transfers between devices: 73.2 us -> 270 us
  local copies, waits for them, and re-layouts: 25.9 us -> 42.6 us
    ppermute x45, waiting for transfers between devices: 543 us -> 312 us  [move(): return lax.ppermute(block, axis, pairs)]
    ppermute x45, starting transfers between devices: 66.8 us -> 264 us  [move(): return lax.ppermute(block, axis, pairs)]
    unnamed x75 -> x97, local copies, waits for them, and re-layouts: 17.3 us -> 33.9 us
    pallas_call x2 -> x3, Pallas kernels: 32 us -> 33.9 us  [run_pairs(): pl.pallas_call(functools.partial(pairs_kernel, phase, n_left, n_right, fr...]
  transfers between devices with their start and end apart: 46 -> 46, of which waited for: 17 -> 15; matrix products, arithmetic and copies ran while one was open for 2% -> 2% of each run, Pallas kernels for 3% -> 4%
where the time goes in v1:
time: 681 us; the launch traced here: 674 us
  waiting for transfers between devices  312 us (46%)
  starting transfers between devices  270 us (40%)
  local copies, waits for them, and re-layouts  42.6 us (6%)
  Pallas kernels  37.9 us (6%)
  between operations  8.24 us (1%)
    ppermute x45, waiting for transfers between devices, move(): return lax.ppermute(block, axis, pairs)  312 us
    ppermute x45, starting transfers between devices, move(): return lax.ppermute(block, axis, pairs)  264 us
    pallas_call x3, Pallas kernels, run_pairs(): pl.pallas_call(functools.partial(pairs_kernel, phase, n_left, n_right, fr...  33.9 us
    unnamed x97, local copies, waits for them, and re-layouts  33.9 us
  transfers between devices with their start and end apart: 46, of which 15 were waited for; matrix products, arithmetic and copies ran while one was open for 2% of the time, Pallas kernels for 4%

profile of v1, /device:TPU:0, one launch (start us, length us, event | category | flops | bytes accessed | tf_op | source)
XLA Modules:
  0.0 673.9 jit_solution(2027222410673926026)
XLA Ops:
  2.8 4.0 pack.1
  6.8 6.4 all-to-all-start
  13.2 2.2 slice_bitcast_fusion
  17.6 11.0 %collective-permute-start.20 = (f32[1,512,512]{2,1,0:T(8,128)S(1)}, f32[1,512,512]{2,1,0:T(8,128)S(1)}, u32[]{:S(2)}, u32[]{:S(2)}) collective-permute-start(f32[1,512,512]{2,1,0:T(8,128)S(1)} %get-tuple-element.23), channel_id=1, source_target_pairs={{0,8},{4,12},{24,16},{28,20},{1,9},{5,13},{25,17},{29,21},{2,10},{... | collective-permute-start | bytes 3145736 | tf_op jit(solution)/shard_map/ppermute | solution.py:213
  28.6 1.4 collective-permute-start.21
  30.0 195.5 %collective-permute-start.12 = (f32[1,512,512]{2,1,0:T(8,128)S(1)}, f32[1,512,512]{2,1,0:T(8,128)S(1)}, u32[]{:S(2)}, u32[]{:S(2)}) collective-permute-start(f32[1,512,512]{2,1,0:T(8,128)S(1)} %get-tuple-element.22), channel_id=1, source_target_pairs={{0,8},{4,12},{24,16},{28,20},{1,9},{5,13},{25,17},{29,21},{2,10},{... | collective-permute-start | bytes 3145736 | tf_op jit(solution)/shard_map/ppermute | solution.py:213
  225.5 1.3 collective-permute-start.35
  226.8 1.3 collective-permute-start.36
  228.1 1.3 collective-permute-start.37
  230.2 16.8 %collective-permute-done.12.refs_14_.refs_22_ = f32[1,512,512]{2,1,0:T(8,128)S(1)} collective-permute-done((f32[1,512,512]{2,1,0:T(8,128)S(1)}, f32[1,512,512]{2,1,0:T(8,128)S(1)}, u32[]{:S(2)}, u32[]{:S(2)}) %collective-permute-start.12) | collective-permute-done | bytes 1048608 | tf_op jit(solution)/shard_map/ppermute | solution.py:213
  247.7 21.9 %collective-permute-done.35.refs_24_.refs_36_ = f32[1,512,512]{2,1,0:T(8,128)S(1)} collective-permute-done((f32[1,512,512]{2,1,0:T(8,128)S(1)}, f32[1,512,512]{2,1,0:T(8,128)S(1)}, u32[]{:S(2)}, u32[]{:S(2)}) %collective-permute-start.35) | collective-permute-done | bytes 1048608 | tf_op jit(solution)/shard_map/ppermute | solution.py:213
  270.3 22.9 %collective-permute-done.36.refs_25_.refs_37_ = f32[1,512,512]{2,1,0:T(8,128)S(1)} collective-permute-done((f32[1,512,512]{2,1,0:T(8,128)S(1)}, f32[1,512,512]{2,1,0:T(8,128)S(1)}, u32[]{:S(2)}, u32[]{:S(2)}) %collective-permute-start.36) | collective-permute-done | bytes 1048608 | tf_op jit(solution)/shard_map/ppermute | solution.py:213
  293.2 1.3 collective-permute-start.18
  294.4 21.2 %collective-permute-done.37.refs_26_.refs_38_ = f32[1,512,512]{2,1,0:T(8,128)S(1)} collective-permute-done((f32[1,512,512]{2,1,0:T(8,128)S(1)}, f32[1,512,512]{2,1,0:T(8,128)S(1)}, u32[]{:S(2)}, u32[]{:S(2)}) %collective-permute-start.37) | collective-permute-done | bytes 1048608 | tf_op jit(solution)/shard_map/ppermute | solution.py:213
  329.1 1.6 collective-permute-start.13
  332.6 1.9 collective-permute-start.40
  335.6 2.4 collective-permute-start.41
  338.1 2.4 collective-permute-start.42
  340.5 1.3 collective-permute-start.38
  341.9 1.3 collective-permute-start.39
  343.2 38.8 %collective-permute-done.18.refs_10_.refs_18_ = f32[3,512,512]{2,1,0:T(8,128)} collective-permute-done((f32[3,512,512]{2,1,0:T(8,128)}, f32[3,512,512]{2,1,0:T(8,128)}, u32[]{:S(2)}, u32[]{:S(2)}) %collective-permute-start.18) | collective-permute-done | bytes 3145760 | tf_op jit(solution)/shard_map/ppermute | solution.py:213
  382.0 1.9 collective-permute-start.19
  384.7 41.2 %collective-permute-done.38.refs_39_ = f32[1,512,512]{2,1,0:T(8,128)} collective-permute-done((f32[1,512,512]{2,1,0:T(8,128)S(1)}, f32[1,512,512]{2,1,0:T(8,128)}, u32[]{:S(2)}, u32[]{:S(2)}) %collective-permute-start.38) | collective-permute-done | bytes 1048608 | tf_op jit(solution)/shard_map/ppermute | solution.py:213
  426.6 20.7 %collective-permute-done.39.refs_40_ = f32[1,512,512]{2,1,0:T(8,128)} collective-permute-done((f32[1,512,512]{2,1,0:T(8,128)S(1)}, f32[1,512,512]{2,1,0:T(8,128)}, u32[]{:S(2)}, u32[]{:S(2)}) %collective-permute-start.39) | collective-permute-done | bytes 1048608 | tf_op jit(solution)/shard_map/ppermute | solution.py:213
  447.3 1.3 collective-permute-start.15
  448.7 1.9 collective-permute-start.43
  450.6 2.4 collective-permute-start.44
  462.3 3.6 constant_dynamic-slice_fusion
  465.9 7.8 %collective-permute-done.15.refs_18_ = f32[1,512,512]{2,1,0:T(8,128)} collective-permute-done((f32[1,512,512]{2,1,0:T(8,128)}, f32[1,512,512]{2,1,0:T(8,128)}, u32[]{:S(2)}, u32[]{:S(2)}) %collective-permute-start.15) | collective-permute-done | bytes 1048608 | tf_op jit(solution)/shard_map/ppermute | solution.py:213
  473.7 1.5 collective-permute-start
  475.7 1.5 collective-permute-start.2
  477.7 1.3 collective-permute-start.4
  479.0 20.9 %collective-permute-done.refs_4_ = f32[1,512,512]{2,1,0:T(8,128)S(1)} collective-permute-done((f32[1,512,512]{2,1,0:T(8,128)}, f32[1,512,512]{2,1,0:T(8,128)S(1)}, u32[]{:S(2)}, u32[]{:S(2)}) %collective-permute-start) | collective-permute-done | bytes 1048608 | tf_op jit(solution)/shard_map/ppermute | solution.py:213
  499.9 1.3 collective-permute-start.5
  501.2 21.2 %collective-permute-done.1.refs_5_ = f32[1,512,512]{2,1,0:T(8,128)S(1)} collective-permute-done((f32[1,512,512]{2,1,0:T(8,128)S(1)}, f32[1,512,512]{2,1,0:T(8,128)S(1)}, u32[]{:S(2)}, u32[]{:S(2)}) %collective-permute-start.1) | collective-permute-done | bytes 1048608 | tf_op jit(solution)/shard_map/ppermute | solution.py:213
  522.4 1.3 collective-permute-start.6
  523.7 21.3 %collective-permute-done.2.refs_6_ = f32[1,512,512]{2,1,0:T(8,128)} collective-permute-done((f32[1,512,512]{2,1,0:T(8,128)S(1)}, f32[1,512,512]{2,1,0:T(8,128)}, u32[]{:S(2)}, u32[]{:S(2)}) %collective-permute-start.2) | collective-permute-done | bytes 1048608 | tf_op jit(solution)/shard_map/ppermute | solution.py:213
  545.0 1.3 collective-permute-start.7
  546.2 18.3 %collective-permute-done.3.refs_7_ = f32[1,512,512]{2,1,0:T(8,128)S(1)} collective-permute-done((f32[1,512,512]{2,1,0:T(8,128)S(1)}, f32[1,512,512]{2,1,0:T(8,128)S(1)}, u32[]{:S(2)}, u32[]{:S(2)}) %collective-permute-start.3) | collective-permute-done | bytes 1048608 | tf_op jit(solution)/shard_map/ppermute | solution.py:213
  564.6 4.4 collective-permute-start.10
  570.1 2.3 collective-permute-start.11
  572.3 2.3 collective-permute-start.8
  574.6 2.3 collective-permute-start.9
  577.0 1.9 compare_select_fusion.2
  579.7 12.1 %collective-permute-done.10.refs_14_ = f32[1,512,512]{2,1,0:T(8,128)} collective-permute-done((f32[1,512,512]{2,1,0:T(8,128)}, f32[1,512,512]{2,1,0:T(8,128)}, u32[]{:S(2)}, u32[]{:S(2)}) %collective-permute-start.10) | collective-permute-done | bytes 1048608 | tf_op jit(solution)/shard_map/ppermute | solution.py:213
  591.8 1.9 collective-permute-start.16
  594.9 1.2 copy-done.3
  596.2 1.2 copy-done.5
  597.4 1.2 copy-done.7
  598.6 1.2 copy-done.9
  599.8 1.2 copy-done.11
  601.1 1.2 copy-done.13
  602.3 1.2 copy-done.15
  603.5 1.2 copy-done.17
  604.7 1.2 copy-done.19
  606.0 1.2 copy-done.21
  609.6 1.2 copy-done.27
  610.9 1.2 copy-done.30
  612.1 1.2 copy-done.33
  613.3 15.7 %shard_map.64.refs_46_ = f32[4,512,512]{2,1,0:T(8,128)} custom-call(s32[6,36]{1,0:T(8,128)S(1)} %stack.2.table, f32[1,512,512]{2,1,0:T(8,128)} %get-tuple-element.20.refs_0_, f32[1,512,512]{2,1,0:T(8,128)S(1)} %get-tuple-element.19.refs_1_, f32[1,512,512]{2,1,0:T(8,128)S(1)} %get-tuple-element.18.refs_2_, f32[1,512,512]{2,1,0:T(8,128)S(1)} %get-tuple-element.17.refs_3_, ...), custom_call_target="tpu_custom_call" | custom-call | flops 8053063680 | bytes 20971520 | tf_op jit(solution)/shard_map/pallas_call | solution.py:115
  629.0 7.7 %collective-permute-done.8.refs_12_ = f32[1,512,512]{2,1,0:T(8,128)} collective-permute-done((f32[1,512,512]{2,1,0:T(8,128)}, f32[1,512,512]{2,1,0:T(8,128)}, u32[]{:S(2)}, u32[]{:S(2)}) %collective-permute-start.8) | collective-permute-done | bytes 1048608 | tf_op jit(solution)/shard_map/ppermute | solution.py:213
  636.7 18.9 %collective-permute-done.9.refs_13_ = f32[1,512,512]{2,1,0:T(8,128)} collective-permute-done((f32[1,512,512]{2,1,0:T(8,128)}, f32[1,512,512]{2,1,0:T(8,128)}, u32[]{:S(2)}, u32[]{:S(2)}) %collective-permute-start.9) | collective-permute-done | bytes 1048608 | tf_op jit(solution)/shard_map/ppermute | solution.py:213
  655.6 13.7 %shard_map.65.refs_20_ = f32[4,512,512]{2,1,0:T(8,128)} custom-call(s32[6,36]{1,0:T(8,128)S(1)} %stack.2.table, f32[1,512,512]{2,1,0:T(8,128)} %get-tuple-element.20.refs_0_, f32[1,512,512]{2,1,0:T(8,128)S(1)} %get-tuple-element.19.refs_1_, f32[1,512,512]{2,1,0:T(8,128)S(1)} %get-tuple-element.18.refs_2_, ...), custom_call_target="tpu_custom_call", output_to_operand_aliasing={{}: (47, {})} | custom-call | flops 8053063680 | bytes 20971520 | tf_op jit(solution)/shard_map/pallas_call | solution.py:115
  669.3 4.6 shard_map.66
  (148 shorter events, 33.4 us)
Async XLA Ops:
  6.8 446.2 %all-to-all-start = ((f32[8,520,512]{2,1,0:T(8,128)}), f32[8,520,512]{2,1,0:T(8,128)}, u32[]{:S(2)}, u32[]{:S(2)}) async-start(f32[8,520,512]{2,1,0:T(8,128)} %pack.1), calls=%async_computation | async-start | bytes 17039360 | tf_op jit(solution)/shard_map/all_to_all | solution.py:220
  15.4 14.6 %collective-permute-start.25 = (f32[1,512,512]{2,1,0:T(8,128)S(1)}, f32[1,512,512]{2,1,0:T(8,128)S(1)}, u32[]{:S(2)}, u32[]{:S(2)}) collective-permute-start(f32[1,512,512]{2,1,0:T(8,128)S(1)} %get-tuple-element.23), channel_id=1, source_target_pairs={{8,16},{12,20},{16,8},{20,12},{9,17},{13,21},{17,9},{21,13},{10,18... | collective-permute-start | bytes 3145736 | tf_op jit(solution)/shard_map/ppermute | solution.py:213
  16.1 209.3 %collective-permute-start.26 = (f32[1,512,512]{2,1,0:T(8,128)S(1)}, f32[1,512,512]{2,1,0:T(8,128)S(1)}, u32[]{:S(2)}, u32[]{:S(2)}) collective-permute-start(f32[1,512,512]{2,1,0:T(8,128)S(1)} %get-tuple-element.21), channel_id=1, source_target_pairs={{8,16},{12,20},{16,8},{20,12},{9,17},{13,21},{17,9},{21,13},{10,18... | collective-permute-start | bytes 3145736 | tf_op jit(solution)/shard_map/ppermute | solution.py:213
  16.9 209.9 %collective-permute-start.27 = (f32[1,512,512]{2,1,0:T(8,128)S(1)}, f32[1,512,512]{2,1,0:T(8,128)S(1)}, u32[]{:S(2)}, u32[]{:S(2)}) collective-permute-start(f32[1,512,512]{2,1,0:T(8,128)S(1)} %get-tuple-element.22), channel_id=1, source_target_pairs={{8,16},{12,20},{16,8},{20,12},{9,17},{13,21},{17,9},{21,13},{10,18... | collective-permute-start | bytes 3145736 | tf_op jit(solution)/shard_map/ppermute | solution.py:213
  17.6 210.5 %collective-permute-start.20 = (f32[1,512,512]{2,1,0:T(8,128)S(1)}, f32[1,512,512]{2,1,0:T(8,128)S(1)}, u32[]{:S(2)}, u32[]{:S(2)}) collective-permute-start(f32[1,512,512]{2,1,0:T(8,128)S(1)} %get-tuple-element.23), channel_id=1, source_target_pairs={{0,8},{4,12},{24,16},{28,20},{1,9},{5,13},{25,17},{29,21},{2,10},{... | collective-permute-start | bytes 3145736 | tf_op jit(solution)/shard_map/ppermute | solution.py:213
  28.6 200.8 %collective-permute-start.21 = (f32[1,512,512]{2,1,0:T(8,128)S(1)}, f32[1,512,512]{2,1,0:T(8,128)S(1)}, u32[]{:S(2)}, u32[]{:S(2)}) collective-permute-start(f32[1,512,512]{2,1,0:T(8,128)S(1)} %get-tuple-element.21), channel_id=1, source_target_pairs={{0,8},{4,12},{24,16},{28,20},{1,9},{5,13},{25,17},{29,21},{2,10},{... | collective-permute-start | bytes 3145736 | tf_op jit(solution)/shard_map/ppermute | solution.py:213
  30.0 216.9 %collective-permute-start.12 = (f32[1,512,512]{2,1,0:T(8,128)S(1)}, f32[1,512,512]{2,1,0:T(8,128)S(1)}, u32[]{:S(2)}, u32[]{:S(2)}) collective-permute-start(f32[1,512,512]{2,1,0:T(8,128)S(1)} %get-tuple-element.22), channel_id=1, source_target_pairs={{0,8},{4,12},{24,16},{28,20},{1,9},{5,13},{25,17},{29,21},{2,10},{... | collective-permute-start | bytes 3145736 | tf_op jit(solution)/shard_map/ppermute | solution.py:213
  225.5 44.0 %collective-permute-start.35 = (f32[1,512,512]{2,1,0:T(8,128)S(1)}, f32[1,512,512]{2,1,0:T(8,128)S(1)}, u32[]{:S(2)}, u32[]{:S(2)}) collective-permute-start(f32[1,512,512]{2,1,0:T(8,128)S(1)} %collective-permute-done.25.refs_18_.refs_26_), channel_id=1, source_target_pairs={{8,0},{12,4},{16,24},{20,28},{9,1},{13,5},{17,25},{21,29},{10,2},{... | collective-permute-start | bytes 3145736 | tf_op jit(solution)/shard_map/ppermute | solution.py:213
  226.8 66.4 %collective-permute-start.36 = (f32[1,512,512]{2,1,0:T(8,128)S(1)}, f32[1,512,512]{2,1,0:T(8,128)S(1)}, u32[]{:S(2)}, u32[]{:S(2)}) collective-permute-start(f32[1,512,512]{2,1,0:T(8,128)S(1)} %collective-permute-done.26.refs_19_.refs_27_), channel_id=1, source_target_pairs={{8,0},{12,4},{16,24},{20,28},{9,1},{13,5},{17,25},{21,29},{10,2},{... | collective-permute-start | bytes 3145736 | tf_op jit(solution)/shard_map/ppermute | solution.py:213
  228.1 87.5 %collective-permute-start.37 = (f32[1,512,512]{2,1,0:T(8,128)S(1)}, f32[1,512,512]{2,1,0:T(8,128)S(1)}, u32[]{:S(2)}, u32[]{:S(2)}) collective-permute-start(f32[1,512,512]{2,1,0:T(8,128)S(1)} %collective-permute-done.27.refs_20_.refs_28_), channel_id=1, source_target_pairs={{8,0},{12,4},{16,24},{20,28},{9,1},{13,5},{17,25},{21,29},{10,2},{... | collective-permute-start | bytes 3145736 | tf_op jit(solution)/shard_map/ppermute | solution.py:213
  229.4 87.9 %collective-permute-start.22 = (f32[1,512,512]{2,1,0:T(8,128)S(1)}, f32[1,512,512]{2,1,0:T(8,128)S(1)}, u32[]{:S(2)}, u32[]{:S(2)}) collective-permute-start(f32[1,512,512]{2,1,0:T(8,128)S(1)} %collective-permute-done.20.refs_12_.refs_20_), channel_id=1, source_target_pairs={{8,12},{12,8},{16,20},{20,16},{9,13},{13,9},{17,21},{21,17},{10,14... | collective-permute-start | bytes 3145736 | tf_op jit(solution)/shard_map/ppermute | solution.py:213
  246.9 73.1 %collective-permute-start.23 = (f32[1,512,512]{2,1,0:T(8,128)S(1)}, f32[1,512,512]{2,1,0:T(8,128)S(1)}, u32[]{:S(2)}, u32[]{:S(2)}) collective-permute-start(f32[1,512,512]{2,1,0:T(8,128)S(1)} %collective-permute-done.21.refs_13_.refs_21_), channel_id=1, source_target_pairs={{8,12},{12,8},{16,20},{20,16},{9,13},{13,9},{17,21},{21,17},{10,14... | collective-permute-start | bytes 3145736 | tf_op jit(solution)/shard_map/ppermute | solution.py:213
  269.5 53.2 %collective-permute-start.24 = (f32[1,512,512]{2,1,0:T(8,128)S(1)}, f32[1,512,512]{2,1,0:T(8,128)S(1)}, u32[]{:S(2)}, u32[]{:S(2)}) collective-permute-start(f32[1,512,512]{2,1,0:T(8,128)S(1)} %collective-permute-done.12.refs_14_.refs_22_), channel_id=1, source_target_pairs={{8,12},{12,8},{16,20},{20,16},{9,13},{13,9},{17,21},{21,17},{10,14... | collective-permute-start | bytes 3145736 | tf_op jit(solution)/shard_map/ppermute | solution.py:213
  293.2 47.4 %copy-start.34 = (f32[1,512,512]{2,1,0:T(8,128)}, f32[1,512,512]{2,1,0:T(8,128)S(1)}, u32[]{:S(2)}) copy-start(f32[1,512,512]{2,1,0:T(8,128)S(1)} %collective-permute-done.36.refs_25_.refs_37_) | copy-start | bytes 3145732
  293.2 88.8 %collective-permute-start.18 = (f32[3,512,512]{2,1,0:T(8,128)}, f32[3,512,512]{2,1,0:T(8,128)}, u32[]{:S(2)}, u32[]{:S(2)}) collective-permute-start(f32[3,512,512]{2,1,0:T(8,128)} %bitcast.17.refs_8_.refs_16_), channel_id=1, source_target_pairs={{8,0},{12,4},{16,24},{20,28},{9,1},{13,5},{17,25},{21,29},{10,2},{... | collective-permute-start | bytes 9437192 | tf_op jit(solution)/shard_map/ppermute | solution.py:213
  315.6 26.2 %copy-start.35 = (f32[1,512,512]{2,1,0:T(8,128)}, f32[1,512,512]{2,1,0:T(8,128)S(1)}, u32[]{:S(2)}) copy-start(f32[1,512,512]{2,1,0:T(8,128)S(1)} %collective-permute-done.37.refs_26_.refs_38_) | copy-start | bytes 3145732
  315.6 9.7 %collective-permute-start.30 = (f32[1,512,512]{2,1,0:T(8,128)S(1)}, f32[1,512,512]{2,1,0:T(8,128)S(1)}, u32[]{:S(2)}, u32[]{:S(2)}) collective-permute-start(f32[1,512,512]{2,1,0:T(8,128)S(1)} %collective-permute-done.25.refs_18_.refs_26_), channel_id=1, source_target_pairs={{8,12},{12,8},{16,20},{20,16},{9,13},{13,9},{17,21},{21,17},{10,14... | collective-permute-start | bytes 3145736 | tf_op jit(solution)/shard_map/ppermute | solution.py:213
  318.3 9.7 %collective-permute-start.31 = (f32[1,512,512]{2,1,0:T(8,128)S(1)}, f32[1,512,512]{2,1,0:T(8,128)S(1)}, u32[]{:S(2)}, u32[]{:S(2)}) collective-permute-start(f32[1,512,512]{2,1,0:T(8,128)S(1)} %collective-permute-done.26.refs_19_.refs_27_), channel_id=1, source_target_pairs={{8,12},{12,8},{16,20},{20,16},{9,13},{13,9},{17,21},{21,17},{10,14... | collective-permute-start | bytes 3145736 | tf_op jit(solution)/shard_map/ppermute | solution.py:213
  321.0 10.7 %collective-permute-start.32 = (f32[1,512,512]{2,1,0:T(8,128)S(1)}, f32[1,512,512]{2,1,0:T(8,128)S(1)}, u32[]{:S(2)}, u32[]{:S(2)}) collective-permute-start(f32[1,512,512]{2,1,0:T(8,128)S(1)} %collective-permute-done.27.refs_20_.refs_28_), channel_id=1, source_target_pairs={{8,12},{12,8},{16,20},{20,16},{9,13},{13,9},{17,21},{21,17},{10,14... | collective-permute-start | bytes 3145736 | tf_op jit(solution)/shard_map/ppermute | solution.py:213
  323.7 11.9 %collective-permute-start.28 = (f32[1,512,512]{2,1,0:T(8,128)S(1)}, f32[1,512,512]{2,1,0:T(8,128)S(1)}, u32[]{:S(2)}, u32[]{:S(2)}) collective-permute-start(f32[1,512,512]{2,1,0:T(8,128)S(1)} %collective-permute-done.20.refs_12_.refs_20_), channel_id=1, source_target_pairs={{8,16},{12,20},{16,8},{20,12},{9,17},{13,21},{17,9},{21,13},{10,18... | collective-permute-start | bytes 3145736 | tf_op jit(solution)/shard_map/ppermute | solution.py:213
  326.3 11.7 %collective-permute-start.29 = (f32[1,512,512]{2,1,0:T(8,128)S(1)}, f32[1,512,512]{2,1,0:T(8,128)S(1)}, u32[]{:S(2)}, u32[]{:S(2)}) collective-permute-start(f32[1,512,512]{2,1,0:T(8,128)S(1)} %collective-permute-done.21.refs_13_.refs_21_), channel_id=1, source_target_pairs={{8,16},{12,20},{16,8},{20,12},{9,17},{13,21},{17,9},{21,13},{10,18... | collective-permute-start | bytes 3145736 | tf_op jit(solution)/shard_map/ppermute | solution.py:213
  329.1 9.0 %collective-permute-start.13 = (f32[1,512,512]{2,1,0:T(8,128)S(1)}, f32[1,512,512]{2,1,0:T(8,128)}, u32[]{:S(2)}, u32[]{:S(2)}) collective-permute-start(f32[1,512,512]{2,1,0:T(8,128)S(1)} %collective-permute-done.12.refs_14_.refs_22_), channel_id=1, source_target_pairs={{8,16},{12,20},{16,8},{20,12},{9,17},{13,21},{17,9},{21,13},{10,18... | collective-permute-start | bytes 3145736 | tf_op jit(solution)/shard_map/ppermute | solution.py:213
  332.6 7.9 %collective-permute-start.40 = (f32[1,512,512]{2,1,0:T(8,128)S(1)}, f32[1,512,512]{2,1,0:T(8,128)S(1)}, u32[]{:S(2)}, u32[]{:S(2)}) collective-permute-start(f32[1,512,512]{2,1,0:T(8,128)S(1)} %collective-permute-done.35.refs_24_.refs_36_), channel_id=1, source_target_pairs={{0,4},{4,0},{24,28},{28,24},{1,5},{5,1},{25,29},{29,25},{2,6},{6,2... | collective-permute-start | bytes 3145736 | tf_op jit(solution)/shard_map/ppermute | solution.py:213
  335.6 90.3 %copy-start.39 = (f32[1,512,512]{2,1,0:T(8,128)}, f32[1,512,512]{2,1,0:T(8,128)S(1)}, u32[]{:S(2)}) copy-start(f32[1,512,512]{2,1,0:T(8,128)S(1)} %collective-permute-done.28.refs_29_) | copy-start | bytes 3145732
  335.6 6.2 collective-permute-start.41
  338.0 110.6 %copy-start.40 = (f32[1,512,512]{2,1,0:T(8,128)}, f32[1,512,512]{2,1,0:T(8,128)S(1)}, u32[]{:S(2)}) copy-start(f32[1,512,512]{2,1,0:T(8,128)S(1)} %collective-permute-done.29.refs_30_) | copy-start | bytes 3145732
  338.0 137.2 %collective-permute-start.17 = (f32[3,512,512]{2,1,0:T(8,128)}, f32[3,512,512]{2,1,0:T(8,128)}, u32[]{:S(2)}, u32[]{:S(2)}) collective-permute-start(f32[3,512,512]{2,1,0:T(8,128)} %bitcast.17.refs_8_.refs_16_), channel_id=1, source_target_pairs={{0,4},{4,0},{8,12},{12,8},{16,20},{20,16},{24,28},{28,24},{1,5},{5... | collective-permute-start | bytes 9437192 | tf_op jit(solution)/shard_map/ppermute | solution.py:213
  338.1 45.8 %collective-permute-start.42 = (f32[1,512,512]{2,1,0:T(8,128)S(1)}, f32[1,512,512]{2,1,0:T(8,128)S(1)}, u32[]{:S(2)}, u32[]{:S(2)}) collective-permute-start(f32[1,512,512]{2,1,0:T(8,128)S(1)} %collective-permute-done.37.refs_26_.refs_38_), channel_id=1, source_target_pairs={{0,4},{4,0},{24,28},{28,24},{1,5},{5,1},{25,29},{29,25},{2,6},{6,2... | collective-permute-start | bytes 3145736 | tf_op jit(solution)/shard_map/ppermute | solution.py:213
  340.5 43.4 %copy-start.36 = (f32[1,512,512]{2,1,0:T(8,128)}, f32[1,512,512]{2,1,0:T(8,128)S(1)}, u32[]{:S(2)}) copy-start(f32[1,512,512]{2,1,0:T(8,128)S(1)} %collective-permute-done.40.refs_27_.refs_41_) | copy-start | bytes 3145732
  340.5 85.4 %collective-permute-start.38 = (f32[1,512,512]{2,1,0:T(8,128)S(1)}, f32[1,512,512]{2,1,0:T(8,128)}, u32[]{:S(2)}, u32[]{:S(2)}) collective-permute-start(f32[1,512,512]{2,1,0:T(8,128)S(1)} %collective-permute-done.28.refs_29_), channel_id=1, source_target_pairs={{8,0},{12,4},{16,24},{20,28},{9,1},{13,5},{17,25},{21,29},{10,2},{... | collective-permute-start | bytes 3145736 | tf_op jit(solution)/shard_map/ppermute | solution.py:213
  341.8 42.8 %copy-start.37 = (f32[1,512,512]{2,1,0:T(8,128)}, f32[1,512,512]{2,1,0:T(8,128)S(1)}, u32[]{:S(2)}) copy-start(f32[1,512,512]{2,1,0:T(8,128)S(1)} %collective-permute-done.41.refs_28_.refs_42_) | copy-start | bytes 3145732
  341.9 105.5 %collective-permute-start.39 = (f32[1,512,512]{2,1,0:T(8,128)S(1)}, f32[1,512,512]{2,1,0:T(8,128)}, u32[]{:S(2)}, u32[]{:S(2)}) collective-permute-start(f32[1,512,512]{2,1,0:T(8,128)S(1)} %collective-permute-done.29.refs_30_), channel_id=1, source_target_pairs={{8,0},{12,4},{16,24},{20,28},{9,1},{13,5},{17,25},{21,29},{10,2},{... | collective-permute-start | bytes 3145736 | tf_op jit(solution)/shard_map/ppermute | solution.py:213
  382.0 95.7 %collective-permute-start.19 = (f32[3,512,512]{2,1,0:T(8,128)}, f32[3,512,512]{2,1,0:T(8,128)}, u32[]{:S(2)}, u32[]{:S(2)}) collective-permute-start(f32[3,512,512]{2,1,0:T(8,128)} %collective-permute-done.18.refs_10_.refs_18_), channel_id=1, source_target_pairs={{0,4},{4,0},{24,28},{28,24},{1,5},{5,1},{25,29},{29,25},{2,6},{6,2... | collective-permute-start | bytes 9437192 | tf_op jit(solution)/shard_map/ppermute | solution.py:213
  383.9 77.7 %copy-start.38 = (f32[1,512,512]{2,1,0:T(8,128)}, f32[1,512,512]{2,1,0:T(8,128)S(1)}, u32[]{:S(2)}) copy-start(f32[1,512,512]{2,1,0:T(8,128)S(1)} %collective-permute-done.42.refs_29_.refs_43_) | copy-start | bytes 3145732
  383.9 64.7 %collective-permute-start.33 = (f32[1,512,512]{2,1,0:T(8,128)S(1)}, f32[1,512,512]{2,1,0:T(8,128)S(1)}, u32[]{:S(2)}, u32[]{:S(2)}) collective-permute-start(f32[1,512,512]{2,1,0:T(8,128)S(1)} %collective-permute-done.28.refs_29_), channel_id=1, source_target_pairs={{8,12},{12,8},{16,20},{20,16},{9,13},{13,9},{17,21},{21,17},{10,14... | collective-permute-start | bytes 3145736 | tf_op jit(solution)/shard_map/ppermute | solution.py:213
  425.9 24.7 %collective-permute-start.34 = (f32[1,512,512]{2,1,0:T(8,128)S(1)}, f32[1,512,512]{2,1,0:T(8,128)S(1)}, u32[]{:S(2)}, u32[]{:S(2)}) collective-permute-start(f32[1,512,512]{2,1,0:T(8,128)S(1)} %collective-permute-done.29.refs_30_), channel_id=1, source_target_pairs={{8,12},{12,8},{16,20},{20,16},{9,13},{13,9},{17,21},{21,17},{10,14... | collective-permute-start | bytes 3145736 | tf_op jit(solution)/shard_map/ppermute | solution.py:213
  447.3 26.3 %collective-permute-start.15 = (f32[1,512,512]{2,1,0:T(8,128)}, f32[1,512,512]{2,1,0:T(8,128)}, u32[]{:S(2)}, u32[]{:S(2)}) collective-permute-start(f32[1,512,512]{2,1,0:T(8,128)} %collective-permute-done.13.refs_16_), channel_id=1, source_target_pairs={{8,0},{12,4},{16,24},{20,28},{9,1},{13,5},{17,25},{21,29},{10,2},{... | collective-permute-start | bytes 3145736 | tf_op jit(solution)/shard_map/ppermute | solution.py:213
  448.6 13.0 %copy-start.41 = (f32[1,512,512]{2,1,0:T(8,128)}, f32[1,512,512]{2,1,0:T(8,128)S(1)}, u32[]{:S(2)}) copy-start(f32[1,512,512]{2,1,0:T(8,128)S(1)} %collective-permute-done.33.refs_34_) | copy-start | bytes 3145732
  448.7 27.0 %collective-permute-start.43 = (f32[1,512,512]{2,1,0:T(8,128)}, f32[1,512,512]{2,1,0:T(8,128)}, u32[]{:S(2)}, u32[]{:S(2)}) collective-permute-start(f32[1,512,512]{2,1,0:T(8,128)} %collective-permute-done.38.refs_39_), channel_id=1, source_target_pairs={{0,4},{4,0},{24,28},{28,24},{1,5},{5,1},{25,29},{29,25},{2,6},{6,2... | collective-permute-start | bytes 3145736 | tf_op jit(solution)/shard_map/ppermute | solution.py:213
  450.6 11.0 %copy-start.42 = (f32[1,512,512]{2,1,0:T(8,128)}, f32[1,512,512]{2,1,0:T(8,128)S(1)}, u32[]{:S(2)}) copy-start(f32[1,512,512]{2,1,0:T(8,128)S(1)} %collective-permute-done.34.refs_35_) | copy-start | bytes 3145732
  450.6 26.6 %collective-permute-start.44 = (f32[1,512,512]{2,1,0:T(8,128)}, f32[1,512,512]{2,1,0:T(8,128)}, u32[]{:S(2)}, u32[]{:S(2)}) collective-permute-start(f32[1,512,512]{2,1,0:T(8,128)} %collective-permute-done.39.refs_40_), channel_id=1, source_target_pairs={{0,4},{4,0},{24,28},{28,24},{1,5},{5,1},{25,29},{29,25},{2,6},{6,2... | collective-permute-start | bytes 3145736 | tf_op jit(solution)/shard_map/ppermute | solution.py:213
  462.2 106.7 %copy-start.44 = (s32[1,1,3,12,3]{3,1,4,2,0:T(1,128)S(1)}, s32[1,1,3,12,3]{3,1,4,2,0:T(1,128)}, u32[]{:S(2)}) copy-start(s32[1,1,3,12,3]{3,1,4,2,0:T(1,128)} %param.12) | copy-start | bytes 1300
  462.2 106.8 %copy-start.43 = (s32[1,1,3]{2,1,0:T(1,128)S(1)}, s32[1,1,3]{2,1,0:T(1,128)}, u32[]{:S(2)}) copy-start(s32[1,1,3]{2,1,0:T(1,128)} %param.13) | copy-start | bytes 40
  462.3 114.7 %copy-start.45 = (pred[36]{0:T(512)(128)(4,1)S(1)}, pred[36]{0:T(512)(128)(4,1)}, u32[]{:S(2)}) copy-start(pred[36]{0:T(512)(128)(4,1)} %constant.228) | copy-start | bytes 112
  462.3 114.7 %copy-start.46 = (pred[36]{0:T(512)(128)(4,1)S(1)}, pred[36]{0:T(512)(128)(4,1)}, u32[]{:S(2)}) copy-start(pred[36]{0:T(512)(128)(4,1)} %constant.229) | copy-start | bytes 112
  473.7 26.2 %collective-permute-start = (f32[1,512,512]{2,1,0:T(8,128)}, f32[1,512,512]{2,1,0:T(8,128)S(1)}, u32[]{:S(2)}, u32[]{:S(2)}) collective-permute-start(f32[1,512,512]{2,1,0:T(8,128)} %get-tuple-element.20.refs_0_), channel_id=1, source_target_pairs={{2,0},{3,1},{0,2},{1,3},{6,4},{7,5},{4,6},{5,7},{10,8},{11,9},{8,1... | collective-permute-start | bytes 3145736 | tf_op jit(solution)/shard_map/ppermute | solution.py:213
  475.2 47.2 %collective-permute-start.1 = (f32[1,512,512]{2,1,0:T(8,128)S(1)}, f32[1,512,512]{2,1,0:T(8,128)S(1)}, u32[]{:S(2)}, u32[]{:S(2)}) collective-permute-start(f32[1,512,512]{2,1,0:T(8,128)S(1)} %get-tuple-element.19.refs_1_), channel_id=1, source_target_pairs={{2,0},{3,1},{0,2},{1,3},{6,4},{7,5},{4,6},{5,7},{10,8},{11,9},{8,1... | collective-permute-start | bytes 3145736 | tf_op jit(solution)/shard_map/ppermute | solution.py:213
  475.7 69.3 %collective-permute-start.2 = (f32[1,512,512]{2,1,0:T(8,128)S(1)}, f32[1,512,512]{2,1,0:T(8,128)}, u32[]{:S(2)}, u32[]{:S(2)}) collective-permute-start(f32[1,512,512]{2,1,0:T(8,128)S(1)} %get-tuple-element.18.refs_2_), channel_id=1, source_target_pairs={{2,0},{3,1},{0,2},{1,3},{6,4},{7,5},{4,6},{5,7},{10,8},{11,9},{8,1... | collective-permute-start | bytes 3145736 | tf_op jit(solution)/shard_map/ppermute | solution.py:213
  477.2 87.3 %collective-permute-start.3 = (f32[1,512,512]{2,1,0:T(8,128)S(1)}, f32[1,512,512]{2,1,0:T(8,128)S(1)}, u32[]{:S(2)}, u32[]{:S(2)}) collective-permute-start(f32[1,512,512]{2,1,0:T(8,128)S(1)} %get-tuple-element.17.refs_3_), channel_id=1, source_target_pairs={{2,0},{3,1},{0,2},{1,3},{6,4},{7,5},{4,6},{5,7},{10,8},{11,9},{8,1... | collective-permute-start | bytes 3145736 | tf_op jit(solution)/shard_map/ppermute | solution.py:213
  477.7 92.3 %collective-permute-start.4 = (f32[1,512,512]{2,1,0:T(8,128)}, f32[1,512,512]{2,1,0:T(8,128)}, u32[]{:S(2)}, u32[]{:S(2)}) collective-permute-start(f32[1,512,512]{2,1,0:T(8,128)} %get-tuple-element.20.refs_0_), channel_id=1, source_target_pairs={{1,0},{3,2},{5,4},{7,6},{9,8},{11,10},{13,12},{15,14},{17,16},{19,... | collective-permute-start | bytes 3145736 | tf_op jit(solution)/shard_map/ppermute | solution.py:213
  499.9 64.7 %copy-start.26 = (f32[1,512,512]{2,1,0:T(8,128)}, f32[1,512,512]{2,1,0:T(8,128)S(1)}, u32[]{:S(2)}) copy-start(f32[1,512,512]{2,1,0:T(8,128)S(1)} %collective-permute-done.refs_4_) | copy-start | bytes 3145732
  499.9 72.4 %collective-permute-start.5 = (f32[1,512,512]{2,1,0:T(8,128)S(1)}, f32[1,512,512]{2,1,0:T(8,128)}, u32[]{:S(2)}, u32[]{:S(2)}) collective-permute-start(f32[1,512,512]{2,1,0:T(8,128)S(1)} %get-tuple-element.19.refs_1_), channel_id=1, source_target_pairs={{1,0},{3,2},{5,4},{7,6},{9,8},{11,10},{13,12},{15,14},{17,16},{19,... | collective-permute-start | bytes 3145736 | tf_op jit(solution)/shard_map/ppermute | solution.py:213
  522.4 46.6 %copy-start.29 = (f32[1,512,512]{2,1,0:T(8,128)}, f32[1,512,512]{2,1,0:T(8,128)S(1)}, u32[]{:S(2)}) copy-start(f32[1,512,512]{2,1,0:T(8,128)S(1)} %collective-permute-done.1.refs_5_) | copy-start | bytes 3145732
  522.4 52.2 %collective-permute-start.6 = (f32[1,512,512]{2,1,0:T(8,128)S(1)}, f32[1,512,512]{2,1,0:T(8,128)}, u32[]{:S(2)}, u32[]{:S(2)}) collective-permute-start(f32[1,512,512]{2,1,0:T(8,128)S(1)} %get-tuple-element.18.refs_2_), channel_id=1, source_target_pairs={{1,0},{3,2},{5,4},{7,6},{9,8},{11,10},{13,12},{15,14},{17,16},{19,... | collective-permute-start | bytes 3145736 | tf_op jit(solution)/shard_map/ppermute | solution.py:213
  545.0 34.0 %collective-permute-start.7 = (f32[1,512,512]{2,1,0:T(8,128)S(1)}, f32[1,512,512]{2,1,0:T(8,128)}, u32[]{:S(2)}, u32[]{:S(2)}) collective-permute-start(f32[1,512,512]{2,1,0:T(8,128)S(1)} %get-tuple-element.17.refs_3_), channel_id=1, source_target_pairs={{1,0},{3,2},{5,4},{7,6},{9,8},{11,10},{13,12},{15,14},{17,16},{19,... | collective-permute-start | bytes 3145736 | tf_op jit(solution)/shard_map/ppermute | solution.py:213
  564.6 4.4 copy-start.32
  564.6 27.2 %collective-permute-start.10 = (f32[1,512,512]{2,1,0:T(8,128)}, f32[1,512,512]{2,1,0:T(8,128)}, u32[]{:S(2)}, u32[]{:S(2)}) collective-permute-start(f32[1,512,512]{2,1,0:T(8,128)} %collective-permute-done.2.refs_6_), channel_id=1, source_target_pairs={{0,1},{2,3},{4,5},{6,7},{8,9},{10,11},{12,13},{14,15},{16,17},{18,... | collective-permute-start | bytes 3145736 | tf_op jit(solution)/shard_map/ppermute | solution.py:213
  570.1 59.0 %collective-permute-start.11 = (f32[1,512,512]{2,1,0:T(8,128)}, f32[1,512,512]{2,1,0:T(8,128)}, u32[]{:S(2)}, u32[]{:S(2)}) collective-permute-start(f32[1,512,512]{2,1,0:T(8,128)} %copy-done.32), channel_id=1, source_target_pairs={{0,1},{2,3},{4,5},{6,7},{8,9},{10,11},{12,13},{14,15},{16,17},{18,... | collective-permute-start | bytes 3145736 | tf_op jit(solution)/shard_map/ppermute | solution.py:213
  572.3 64.4 %collective-permute-start.8 = (f32[1,512,512]{2,1,0:T(8,128)}, f32[1,512,512]{2,1,0:T(8,128)}, u32[]{:S(2)}, u32[]{:S(2)}) collective-permute-start(f32[1,512,512]{2,1,0:T(8,128)} %copy-done.26), channel_id=1, source_target_pairs={{0,1},{2,3},{4,5},{6,7},{8,9},{10,11},{12,13},{14,15},{16,17},{18,... | collective-permute-start | bytes 3145736 | tf_op jit(solution)/shard_map/ppermute | solution.py:213
  574.6 81.0 %collective-permute-start.9 = (f32[1,512,512]{2,1,0:T(8,128)}, f32[1,512,512]{2,1,0:T(8,128)}, u32[]{:S(2)}, u32[]{:S(2)}) collective-permute-start(f32[1,512,512]{2,1,0:T(8,128)} %copy-done.29), channel_id=1, source_target_pairs={{0,1},{2,3},{4,5},{6,7},{8,9},{10,11},{12,13},{14,15},{16,17},{18,... | collective-permute-start | bytes 3145736 | tf_op jit(solution)/shard_map/ppermute | solution.py:213
  578.9 90.3 %collective-permute-start.14 = (f32[1,512,512]{2,1,0:T(8,128)}, f32[1,512,512]{2,1,0:T(8,128)S(1)}, u32[]{:S(2)}, u32[]{:S(2)}) collective-permute-start(f32[1,512,512]{2,1,0:T(8,128)} %collective-permute-done.13.refs_16_), channel_id=1, source_target_pairs={{8,12},{12,8},{16,20},{20,16},{9,13},{13,9},{17,21},{21,17},{10,14... | collective-permute-start | bytes 3145736 | tf_op jit(solution)/shard_map/ppermute | solution.py:213
  591.8 77.5 %collective-permute-start.16 = (f32[1,512,512]{2,1,0:T(8,128)}, f32[1,512,512]{2,1,0:T(8,128)S(1)}, u32[]{:S(2)}, u32[]{:S(2)}) collective-permute-start(f32[1,512,512]{2,1,0:T(8,128)} %collective-permute-done.15.refs_18_), channel_id=1, source_target_pairs={{0,4},{4,0},{24,28},{28,24},{1,5},{5,1},{25,29},{29,25},{2,6},{6,2... | collective-permute-start | bytes 3145736 | tf_op jit(solution)/shard_map/ppermute | solution.py:213
  613.3 42.3 %copy-start.31 = (f32[1,512,512]{2,1,0:T(8,128)S(1)}, f32[1,512,512]{2,1,0:T(8,128)}, u32[]{:S(2)}) copy-start(f32[1,512,512]{2,1,0:T(8,128)} %copy-done.29) | copy-start | bytes 3145732
  629.0 40.3 %copy-start.28 = (f32[1,512,512]{2,1,0:T(8,128)S(1)}, f32[1,512,512]{2,1,0:T(8,128)}, u32[]{:S(2)}) copy-start(f32[1,512,512]{2,1,0:T(8,128)} %copy-done.26) | copy-start | bytes 3145732
  (29 other events, 32.4 us)
